TPU v7x, 128 devices: a whole 4x4x4 slice. The times are simulated.
128 devices in a mesh: tm: 16 (over x, y_hi, core), dom: 8 (over z, y_lo).
Axes of the slice: x: 4, y: 4 (y_hi: 2, y_lo: 2; y = y_hi * 2 + y_lo), z: 4, core: 2. Of those that a mesh axis runs over, the one named last changes fastest.
Arguments:
- state_interior: float32 [16, 16384, 128], P('tm', 'dom'), may hold values from -6 to 6
- state_shared: float32 [16, 2048, 128], P('tm'), may hold values from -6 to 6
- gain_interior: float32 [16, 16384], P('tm', 'dom'), may hold values from 0.2 to 0.95
- gain_shared: float32 [16, 2048], P('tm'), may hold values from 0.2 to 0.95
- jac_blocks: float32 [256, 64, 64], P('dom'), may hold values from -1.5 to 10, as said below
- off_blocks: float32 [256, 64, 64], P('dom'), may hold values from -0.6 to 0.6
- block_link: int32 [256], P('dom'), may hold values from 0 to 31
- mass: float32 [16384], P('dom'), may hold values from 0.5 to 4
- shared_mass: float32 [2048], replicated, may hold values from 0.5 to 2
- shared_diag: float32 [2048], replicated, may hold values from 2.5 to 4
- link_node: int32 [4096], P('dom'), may hold values from 0 to 2047
- link_shared: int32 [4096], P('dom'), may hold values from 0 to 2047
- link_cond: float32 [4096], P('dom'), may hold values from 0.5 to 2
- source_amp: float32 [16384, 128], P('dom'), may hold values from -12 to 12
- phase: float32 [16384], P('dom'), may hold values from -3.140625 to 3.140625
- nonlin: float32 [128], replicated, may hold values from 0.1 to 1
Outputs:
- new_interior: float32 [16, 16384, 128], P('tm', 'dom')
- new_shared: float32 [16, 2048, 128], P('tm')
Inputs may be any that keep to these rules, and one draw needn't show every extreme that they name: `jac_blocks`: each block has diagonal entries from 6 to 10 and off-diagonal entries of magnitude at most 1.5.
All inputs are finite; a program needn't handle non-finite values.
Results may differ from a plain program's by a relative error of at most 0.0001.
Values sent between devices are 32-bit elements; how exact they have to be, the bound alone decides.
A program may use at most 128 MiB of HBM per device.

v0:
```python
import math

import jax
import jax.numpy as jnp
from jax import lax
from jax.sharding import PartitionSpec as P

FINE = 2
NEWTON = 2
KRYLOV = 2


def carried_in(value, axis, join, neutral):
    count, mine = (lax.axis_size(axis), lax.axis_index(axis))
    pieces = jax.tree.map(lambda part: lax.all_gather(part, axis), value)
    total = jax.tree.map(
        lambda part, zero: jnp.full_like(part, 0) + jnp.asarray(zero, part.dtype), value, neutral
    )

    def step(position, total):
        longer = join(total, jax.tree.map(lambda part: part[position], pieces))
        return jax.tree.map(lambda new, old: jnp.where(position < mine, new, old), longer, total)

    return lax.fori_loop(0, count - 1, step, total)


def broadcast(block, axis, holder):
    block = jnp.where(lax.axis_index(axis) == holder, block, jnp.zeros_like(block))
    return lax.psum(block, axis)


def rotate_solve(columns, start_norm, krylov):
    cosines = []
    sine_parts = []
    rhs_vals = [start_norm] + [jnp.zeros_like(start_norm) for j in range(krylov)]
    triangle = []
    for j in range(krylov):
        column = list(columns[j])
        for i in range(j):
            upper_entry = cosines[i] * column[i] + sine_parts[i] * column[i + 1]
            lower_entry = -sine_parts[i] * column[i] + cosines[i] * column[i + 1]
            column[i] = upper_entry
            column[i + 1] = lower_entry
        radius = jnp.sqrt(column[j] * column[j] + column[j + 1] * column[j + 1])
        cosine = column[j] / radius
        sine_part = column[j + 1] / radius
        column[j] = radius
        cosines.append(cosine)
        sine_parts.append(sine_part)
        rhs_vals[j + 1] = -sine_part * rhs_vals[j]
        rhs_vals[j] = cosine * rhs_vals[j]
        triangle.append(column[: j + 1])
    coeffs = [None] * krylov
    for j in reversed(range(krylov)):
        partial_rhs = rhs_vals[j]
        for k in range(j + 1, krylov):
            partial_rhs = partial_rhs - triangle[k][j] * coeffs[k]
        coeffs[j] = partial_rhs / triangle[j][j]
    return coeffs


def project_vectors(inner_sums, basis_in, basis_sh, image_in, image_sh):
    heights = inner_sums(basis_in, basis_sh, image_in, image_sh)
    for i in range(len(basis_in)):
        image_in = image_in - heights[i] * basis_in[i]
        image_sh = image_sh - heights[i] * basis_sh[i]
    length = jnp.sqrt(inner_sums([image_in], [image_sh], image_in, image_sh)[0])
    return (heights, image_in, image_sh, length)


def combine_basis(columns, start_norm, basis_in, basis_sh):
    coeffs = rotate_solve(columns, start_norm, KRYLOV)
    step_in = coeffs[0] * basis_in[0]
    step_sh = coeffs[0] * basis_sh[0]
    step_in = step_in + coeffs[1] * basis_in[1]
    step_sh = step_sh + coeffs[1] * basis_sh[1]
    return (step_in, step_sh)


def krylov_solve(operate_on, inner_sums, rhs_in, rhs_sh):
    columns = []
    start_norm = jnp.sqrt(inner_sums([rhs_in], [rhs_sh], rhs_in, rhs_sh)[0] + 1e-30)
    basis_in = [rhs_in / start_norm]
    basis_sh = [rhs_sh / start_norm]
    for j in range(KRYLOV):
        image_in, image_sh = operate_on(basis_in[j], basis_sh[j])
        heights, image_in, image_sh, length = project_vectors(
            inner_sums, basis_in, basis_sh, image_in, image_sh
        )
        columns.append([heights[i] for i in range(j + 1)] + [length])
        if j + 1 < KRYLOV:
            basis_in.append(image_in / length)
            basis_sh.append(image_sh / length)
    return combine_basis(columns, start_norm, basis_in, basis_sh)


def compose_maps(earlier, later):
    return (
        later[0] * earlier[0],
        later[1] * earlier[1],
        later[0][:, None] * earlier[2] + later[2],
        later[1][:, None] * earlier[3] + later[3],
    )


def shards(
    state_interior,
    state_shared,
    gain_interior,
    gain_shared,
    jac_blocks,
    off_blocks,
    block_link,
    mass,
    shared_mass,
    shared_diag,
    link_node,
    link_shared,
    link_cond,
    source_amp,
    phase,
    nonlin,
):
    highest = lax.Precision.HIGHEST
    start_in = state_interior[0]
    start_sh = state_shared[0]
    block_count = jac_blocks.shape[0]
    block_size = jac_blocks.shape[1]
    samples = start_in.shape[1]
    shared_count = start_sh.shape[0]

    def operate_local(vec_in, vec_sh):
        blocked = vec_in.reshape(block_count, block_size, samples)
        block_out = jnp.einsum("bij,bjs->bis", jac_blocks, blocked, precision=highest)
        block_out = block_out + jnp.einsum(
            "bij,bjs->bis", off_blocks, blocked[block_link], precision=highest
        )
        out_in = block_out.reshape(vec_in.shape)
        link_flow = link_cond[:, None] * (vec_in[link_node] - vec_sh[link_shared])
        out_in = out_in.at[link_node].add(link_flow)
        partial_flow = -jax.ops.segment_sum(link_flow, link_shared, num_segments=shared_count)
        return (out_in, partial_flow)

    def operate_on(vec_in, vec_sh):
        out_in, partial_flow = operate_local(vec_in, vec_sh)
        out_sh = lax.psum(partial_flow, "dom") + shared_diag[:, None] * vec_sh
        return (out_in, out_sh)

    def inner_sums(vecs_in, vecs_sh, other_in, other_sh):
        part_in = jnp.stack([jnp.sum(v * other_in, axis=0) for v in vecs_in])
        part_sh = jnp.stack([jnp.sum(v * other_sh, axis=0) for v in vecs_sh])
        return lax.psum(part_in, "dom") + part_sh

    slices = lax.axis_size("tm")
    slice_f = lax.axis_index("tm").astype(jnp.float32)
    old_in, old_sh = (start_in, start_sh)
    for k in range(FINE):
        angle = (slice_f * FINE + (k + 1.0)) * (2.0 * math.pi / (slices * FINE))
        drive = source_amp * jnp.sin(angle + phase)[:, None]
        fixed_in = mass[:, None] * old_in + drive
        fixed_sh = shared_mass[:, None] * old_sh
        guess_in, guess_sh = (old_in, old_sh)
        for m in range(NEWTON):
            lin_in, lin_sh = operate_on(guess_in, guess_sh)
            resid_in = lin_in + nonlin[None, :] * jnp.tanh(guess_in) - fixed_in
            resid_sh = lin_sh - fixed_sh
            step_in, step_sh = krylov_solve(operate_on, inner_sums, -resid_in, -resid_sh)
            guess_in = guess_in + step_in
            guess_sh = guess_sh + step_sh
        old_in, old_sh = (guess_in, guess_sh)
    gain_in = gain_interior[0]
    gain_sh = gain_shared[0]
    jump_in = old_in - gain_in[:, None] * start_in
    jump_sh = old_sh - gain_sh[:, None] * start_sh
    own_map = (gain_in, gain_sh, jump_in, jump_sh)
    identity = (
        jnp.ones_like(gain_in),
        jnp.ones_like(gain_sh),
        jnp.zeros_like(jump_in),
        jnp.zeros_like(jump_sh),
    )
    prefix = carried_in(own_map, "tm", compose_maps, identity)
    closing = compose_maps(prefix, own_map)
    period_map = (
        broadcast(closing[0], "tm", slices - 1),
        broadcast(closing[1], "tm", slices - 1),
        broadcast(closing[2], "tm", slices - 1),
        broadcast(closing[3], "tm", slices - 1),
    )
    first_in = period_map[2] / (1.0 - period_map[0])[:, None]
    first_sh = period_map[3] / (1.0 - period_map[1])[:, None]
    new_in = prefix[0][:, None] * first_in + prefix[2]
    new_sh = prefix[1][:, None] * first_sh + prefix[3]
    return (new_in[None], new_sh[None])


def solution(mesh):
    return jax.shard_map(
        shards,
        mesh=mesh,
        in_specs=(
            P("tm", "dom", None),
            P("tm", None, None),
            P("tm", "dom"),
            P("tm", None),
            P("dom", None, None),
            P("dom", None, None),
            P("dom"),
            P("dom"),
            P(),
            P(),
            P("dom"),
            P("dom"),
            P("dom"),
            P("dom", None),
            P("dom"),
            P(),
        ),
        out_specs=(P("tm", "dom", None), P("tm", None, None)),
        check_vma=False,
    )
```

profile of v0, /device:TPU:1, one launch (start us, length us, event | category | flops | bytes accessed | tf_op | source)
XLA Modules:
  0.0 1763.0 jit_solution(1432945025314656718)
XLA Ops:
  35.2 18.8 %psum.252 = f32[1,128]{1,0:T(1,128)S(1)} all-reduce(f32[1,128]{1,0:T(1,128)S(1)} %bitcast.548), channel_id=1, replica_groups=mesh['tm'=16,'dom'=8] {'dom'}, use_global_device_ids=true, to_apply=%region_2.0 | all-reduce | flops 128 | bytes 1024 | tf_op jit(solution)/shard_map/psum | solution.py:152
  53.9 44.2 %all-reduce.16.cloned.1.call-done = f32[2048,128]{1,0:T(8,128)} async-done(((f32[2048,128]{1,0:T(8,128)}), f32[2048,128]{1,0:T(8,128)}) %all-reduce.16.cloned.1.call-update) | async-done | bytes 1048592 | tf_op jit(solution)/shard_map/psum | solution.py:146
  127.2 15.7 psum.254
  142.9 50.8 %all-reduce.18.cloned.1.call-done = f32[2048,128]{1,0:T(8,128)} async-done(((f32[2048,128]{1,0:T(8,128)}), f32[2048,128]{1,0:T(8,128)}) %all-reduce.18.cloned.1.call-update) | async-done | bytes 1048592 | tf_op jit(solution)/shard_map/psum | solution.py:146
  197.9 14.7 psum.256
  257.7 53.0 %all-reduce.20.cloned.1.call-done = f32[2048,128]{1,0:T(8,128)} async-done(((f32[2048,128]{1,0:T(8,128)}), f32[2048,128]{1,0:T(8,128)}) %all-reduce.20.cloned.1.call-update) | async-done | bytes 1048592 | tf_op jit(solution)/shard_map/psum | solution.py:146
  316.1 14.7 psum.259
  377.0 58.4 %all-reduce.22.cloned.1.call-done = f32[2048,128]{1,0:T(8,128)} async-done(((f32[2048,128]{1,0:T(8,128)}), f32[2048,128]{1,0:T(8,128)}) %all-reduce.22.cloned.1.call-update) | async-done | bytes 1048592 | tf_op jit(solution)/shard_map/psum | solution.py:146
  463.7 15.6 psum.262
  479.3 51.3 %all-reduce.24.cloned.1.call-done = f32[2048,128]{1,0:T(8,128)} async-done(((f32[2048,128]{1,0:T(8,128)}), f32[2048,128]{1,0:T(8,128)}) %all-reduce.24.cloned.1.call-update) | async-done | bytes 1048592 | tf_op jit(solution)/shard_map/psum | solution.py:146
  534.9 14.7 psum.264
  594.7 53.0 %all-reduce.26.cloned.1.call-done = f32[2048,128]{1,0:T(8,128)} async-done(((f32[2048,128]{1,0:T(8,128)}), f32[2048,128]{1,0:T(8,128)}) %all-reduce.26.cloned.1.call-update) | async-done | bytes 1048592 | tf_op jit(solution)/shard_map/psum | solution.py:146
  653.1 14.9 psum.267
  715.0 57.6 %all-reduce.28.cloned.1.call-done = f32[2048,128]{1,0:T(8,128)} async-done(((f32[2048,128]{1,0:T(8,128)}), f32[2048,128]{1,0:T(8,128)}) %all-reduce.28.cloned.1.call-update) | async-done | bytes 1048592 | tf_op jit(solution)/shard_map/psum | solution.py:146
  801.3 15.4 psum.270
  816.7 51.4 %all-reduce.30.cloned.1.call-done = f32[2048,128]{1,0:T(8,128)} async-done(((f32[2048,128]{1,0:T(8,128)}), f32[2048,128]{1,0:T(8,128)}) %all-reduce.30.cloned.1.call-update) | async-done | bytes 1048592 | tf_op jit(solution)/shard_map/psum | solution.py:146
  872.4 14.7 psum.272
  932.2 52.8 %all-reduce.32.cloned.1.call-done = f32[2048,128]{1,0:T(8,128)} async-done(((f32[2048,128]{1,0:T(8,128)}), f32[2048,128]{1,0:T(8,128)}) %all-reduce.32.cloned.1.call-update) | async-done | bytes 1048592 | tf_op jit(solution)/shard_map/psum | solution.py:146
  990.3 14.7 psum.275
  1052.7 57.3 %all-reduce.34.cloned.1.call-done = f32[2048,128]{1,0:T(8,128)} async-done(((f32[2048,128]{1,0:T(8,128)}), f32[2048,128]{1,0:T(8,128)}) %all-reduce.34.cloned.1.call-update) | async-done | bytes 1048592 | tf_op jit(solution)/shard_map/psum | solution.py:146
  1137.9 15.5 psum.278
  1153.5 51.5 %all-reduce.36.cloned.1.call-done = f32[2048,128]{1,0:T(8,128)} async-done(((f32[2048,128]{1,0:T(8,128)}), f32[2048,128]{1,0:T(8,128)}) %all-reduce.36.cloned.1.call-update) | async-done | bytes 1048592 | tf_op jit(solution)/shard_map/psum | solution.py:146
  1209.2 14.7 psum.280
  1269.0 53.0 %all-reduce.38.cloned.1.call-done = f32[2048,128]{1,0:T(8,128)} async-done(((f32[2048,128]{1,0:T(8,128)}), f32[2048,128]{1,0:T(8,128)}) %all-reduce.38.cloned.1.call-update) | async-done | bytes 1048592 | tf_op jit(solution)/shard_map/psum | solution.py:146
  1327.4 14.7 psum.283
  1347.3 32.9 %all-gather.3 = f32[16,1,2048]{2,1,0:T(1,128)S(1)} all-gather(f32[1,1,2048]{2,1,0:T(1,128)S(1)} %bitcast.521), channel_id=1, replica_groups=mesh['tm'=16,'dom'=8] {'tm'}, dimensions={0}, use_global_device_ids=true | all-gather | bytes 139264 | tf_op jit(solution)/shard_map/all_gather | solution.py:15
  1380.2 19.7 %all-gather.2 = f32[16,1,2048]{2,1,0:T(1,128)S(1)} all-gather(f32[1,1,2048]{2,1,0:T(1,128)S(1)} %bitcast.517), channel_id=1, replica_groups=mesh['tm'=16,'dom'=8] {'tm'}, dimensions={0}, use_global_device_ids=true | all-gather | bytes 139264 | tf_op jit(solution)/shard_map/all_gather | solution.py:15
  1399.9 64.2 %all-gather.7.cloned.1.call-done = f32[32768,128]{1,0:T(8,128)} async-done(((f32[2048,128]{1,0:T(8,128)}), f32[32768,128]{1,0:T(8,128)}) %all-gather.7.cloned.1.call-update) | async-done | bytes 16777232 | tf_op jit(solution)/shard_map/all_gather | solution.py:15
  1464.1 110.8 %all-gather.9.cloned.1.call-done = f32[32768,128]{1,0:T(8,128)} async-done(((f32[2048,128]{1,0:T(8,128)}), f32[32768,128]{1,0:T(8,128)}) %all-gather.9.cloned.1.call-update) | async-done | bytes 16777232 | tf_op jit(solution)/shard_map/all_gather | solution.py:15
  1575.0 31.4 %while.20 = (s32[]{:T(128)}, f32[2048]{0:T(1024)S(1)}, f32[2048]{0:T(1024)S(1)}, f32[2048,128]{1,0:T(8,128)S(1)}, f32[2048,128]{1,0:T(8,128)S(1)}, /*index=5*/s3...) while((s32[]{:T(128)}, f32[2048]{0:T(1024)S(1)}, ...), condition=%wide.region_105.106_spmd.clone, body=%wide.region_104.105_spmd.clone.sunk | while | flops 2109444 | bytes 6389911 | solution.py:24
  1609.3 59.8 %all-reduce = (f32[2048]{0:T(1024)S(1)}, f32[2048]{0:T(1024)S(1)}) all-reduce(f32[2048]{0:T(1024)S(1)} %get-tuple-element.324, f32[2048]{0:T(1024)S(1)} %get-tuple-element.323), channel_id=1, replica_groups=mesh['tm'=16,'dom'=8] {'tm'}, use_global_device_ids=true, to_apply=%region_107.108 | all-reduce | flops 4096 | bytes 32768 | tf_op jit(solution)/shard_map/psum | solution.py:29
  1669.0 82.1 %all-reduce.40.cloned.1.call-done = (f32[2048,128]{1,0:T(8,128)}, f32[2048,128]{1,0:T(8,128)}) async-done(((f32[2048,128]{1,0:T(8,128)}, f32[2048,128]{1,0:T(8,128)}), (f32[2048,128]{1,0:T(8,128)}, f32[2048,128]{1,0:T(8,128)})) %all-reduce.40.cloned.1.call-update) | async-done | bytes 2097168 | tf_op jit(solution)/shard_map/psum | solution.py:29
  (316 shorter events, 544.4 us)
Async XLA Ops:
  7.2 13.5 copy-start
  7.2 18.2 %copy-start.3 = (f32[1,2048,128]{2,1,0:T(8,128)S(1)}, f32[1,2048,128]{2,1,0:T(8,128)}, u32[]{:S(2)}) copy-start(f32[1,2048,128]{2,1,0:T(8,128)} %param.18) | copy-start | bytes 3145732
  7.2 19.5 %copy-start.7 = (f32[512]{0:T(512)S(1)}, f32[512]{0:T(512)}, u32[]{:S(2)}) copy-start(f32[512]{0:T(512)} %param.30) | copy-start | bytes 6148
  7.2 18.2 %copy-start.13 = (f32[128]{0:T(128)S(1)}, f32[128]{0:T(128)}, u32[]{:S(2)}) copy-start(f32[128]{0:T(128)} %param.33) | copy-start | bytes 1540
  7.2 25.2 %copy-start.12 = (f32[2048]{0:T(1024)S(1)}, f32[2048]{0:T(1024)}, u32[]{:S(2)}) copy-start(f32[2048]{0:T(1024)} %param.32) | copy-start | bytes 24580
  7.2 25.2 %copy-start.11 = (f32[2048]{0:T(1024)S(1)}, f32[2048]{0:T(1024)}, u32[]{:S(2)}) copy-start(f32[2048]{0:T(1024)} %param.25) | copy-start | bytes 24580
  7.2 90.9 %copy-start.8 = (f32[2048]{0:T(1024)S(1)}, f32[2048]{0:T(1024)}, u32[]{:S(2)}) copy-start(f32[2048]{0:T(1024)} %param.26) | copy-start | bytes 24580
  7.2 90.9 %copy-start.6 = (f32[2048]{0:T(1024)S(1)}, f32[2048]{0:T(1024)}, u32[]{:S(2)}) copy-start(f32[2048]{0:T(1024)} %param.27) | copy-start | bytes 24580
  7.3 90.9 %all-reduce.16.cloned.1.call-start = ((), (), s32[]{:S(2)}) async-start(), calls=%async_computation | async-start | bytes 2097152 | tf_op jit(solution)/shard_map/psum | solution.py:146
  18.1 175.6 %all-reduce.18.cloned.1.call-start = ((), (), s32[]{:S(2)}) async-start(), calls=%async_computation.1 | async-start | bytes 2097152 | tf_op jit(solution)/shard_map/psum | solution.py:146
  25.4 91.2 %copy-start.1 = (f32[32,64,64]{2,1,0:T(8,128)S(1)}, f32[32,64,64]{2,1,0:T(8,128)}, u32[]{:S(2)}) copy-start(f32[32,64,64]{2,1,0:T(8,128)} %param.23) | copy-start | bytes 1572868
  113.3 197.4 %all-reduce.20.cloned.1.call-start = ((), (), s32[]{:S(2)}) async-start(), calls=%async_computation.2 | async-start | bytes 2097152 | tf_op jit(solution)/shard_map/psum | solution.py:146
  227.5 207.9 %all-reduce.22.cloned.1.call-start = ((), (), s32[]{:S(2)}) async-start(), calls=%async_computation.3 | async-start | bytes 2097152 | tf_op jit(solution)/shard_map/psum | solution.py:146
  335.0 20.4 %copy-start.5 = (f32[2048,128]{1,0:T(8,128)S(1)}, f32[2048,128]{1,0:T(8,128)}, u32[]{:S(2)}) copy-start(f32[2048,128]{1,0:T(8,128)} %get-tuple-element.308) | copy-start | bytes 3145732
  352.4 178.3 %all-reduce.24.cloned.1.call-start = ((), (), s32[]{:S(2)}) async-start(), calls=%async_computation.4 | async-start | bytes 2097152 | tf_op jit(solution)/shard_map/psum | solution.py:146
  450.3 197.4 %all-reduce.26.cloned.1.call-start = ((), (), s32[]{:S(2)}) async-start(), calls=%async_computation.5 | async-start | bytes 2097152 | tf_op jit(solution)/shard_map/psum | solution.py:146
  564.5 208.1 %all-reduce.28.cloned.1.call-start = ((), (), s32[]{:S(2)}) async-start(), calls=%async_computation.6 | async-start | bytes 2097152 | tf_op jit(solution)/shard_map/psum | solution.py:146
  672.1 20.2 %copy-start.2 = (f32[2048,128]{1,0:T(8,128)S(1)}, f32[2048,128]{1,0:T(8,128)}, u32[]{:S(2)}) copy-start(f32[2048,128]{1,0:T(8,128)} %get-tuple-element.302) | copy-start | bytes 3145732
  689.5 178.6 %all-reduce.30.cloned.1.call-start = ((), (), s32[]{:S(2)}) async-start(), calls=%async_computation.7 | async-start | bytes 2097152 | tf_op jit(solution)/shard_map/psum | solution.py:146
  787.7 197.3 %all-reduce.32.cloned.1.call-start = ((), (), s32[]{:S(2)}) async-start(), calls=%async_computation.8 | async-start | bytes 2097152 | tf_op jit(solution)/shard_map/psum | solution.py:146
  901.9 208.1 %all-reduce.34.cloned.1.call-start = ((), (), s32[]{:S(2)}) async-start(), calls=%async_computation.9 | async-start | bytes 2097152 | tf_op jit(solution)/shard_map/psum | solution.py:146
  1009.3 100.6 %copy-start.4 = (f32[2048,128]{1,0:T(8,128)S(1)}, f32[2048,128]{1,0:T(8,128)}, u32[]{:S(2)}) copy-start(f32[2048,128]{1,0:T(8,128)} %get-tuple-element.301) | copy-start | bytes 3145732
  1026.8 178.2 %all-reduce.36.cloned.1.call-start = ((), (), s32[]{:S(2)}) async-start(), calls=%async_computation.10 | async-start | bytes 2097152 | tf_op jit(solution)/shard_map/psum | solution.py:146
  1124.6 197.4 %all-reduce.38.cloned.1.call-start = ((), (), s32[]{:S(2)}) async-start(), calls=%async_computation.11 | async-start | bytes 2097152 | tf_op jit(solution)/shard_map/psum | solution.py:146
  1227.5 114.6 %copy-start.9 = (f32[1,2048]{1,0:T(1,128)S(1)}, f32[1,2048]{1,0:T(1,128)}, u32[]{:S(2)}) copy-start(f32[1,2048]{1,0:T(1,128)} %param.20) | copy-start | bytes 24580
  1227.5 114.7 %copy-start.10 = (f32[1,2048]{1,0:T(1,128)S(1)}, f32[1,2048]{1,0:T(1,128)}, u32[]{:S(2)}) copy-start(f32[1,2048]{1,0:T(1,128)} %param.21) | copy-start | bytes 24580
  1238.8 225.4 %all-gather.7.cloned.1.call-start = ((), (), s32[]{:S(2)}) async-start(), calls=%async_computation.12 | async-start | bytes 17825792 | tf_op jit(solution)/shard_map/all_gather | solution.py:15
  1346.6 228.4 %all-gather.9.cloned.1.call-start = ((), (), s32[]{:S(2)}) async-start(), calls=%async_computation.13 | async-start | bytes 17825792 | tf_op jit(solution)/shard_map/all_gather | solution.py:15
  1347.2 404.0 %all-reduce.40.cloned.1.call-start = ((), (), s32[]{:S(2)}) async-start(), calls=%async_computation.14 | async-start | bytes 4194304 | tf_op jit(solution)/shard_map/psum | solution.py:29
Sparse Core Ops, SparseCore 0:
  18.2 79.8 all-reduce.15
  113.5 80.1 all-reduce.17
  227.6 83.0 all-reduce.19
  352.5 82.8 all-reduce.21
  450.5 80.1 all-reduce.23
  564.6 83.0 all-reduce.25
  689.6 82.8 all-reduce.27
  787.9 80.2 all-reduce.29
  902.0 82.9 all-reduce.31
  1026.9 83.0 all-reduce.33
  1124.7 80.2 all-reduce.35
  1238.9 83.0 all-reduce.37
  1346.7 117.3 all-gather.6
  1467.0 107.9 all-gather.8
  1609.4 141.7 all-reduce.39
where the time goes:
time: 1780 us; the launch traced here: 1760 us
  waiting for transfers between devices  892 us (50%)
  blocking collectives  406 us (23%)
  other arithmetic  298 us (17%)
  local copies, waits for them, and re-layouts  85.5 us (5%)
  matrix products  63 us (4%)
    psum x12, waiting for transfers between devices, operate_on(): out_sh = lax.psum(partial_flow, 'dom') + shared_diag[:, None] * vec_sh  634 us
    psum x20, blocking collectives, inner_sums(): return lax.psum(part_in, 'dom') + part_sh  294 us
    all_gather x2, waiting for transfers between devices, carried_in(): pieces = jax.tree.map(lambda part: lax.all_gather(part, axis), value)  175 us
    psum x1, waiting for transfers between devices, broadcast(): return lax.psum(block, axis)  82.1 us
    scatter-add x12, other arithmetic, operate_local(): out_in = out_in.at[link_node].add(link_flow)  68.6 us
    psum x1, blocking collectives, broadcast(): return lax.psum(block, axis)  59.8 us
    gather x24, local copies, waits for them, and re-layouts, operate_local(): link_flow = link_cond[:, None] * (vec_in[link_node] - vec_sh[link_shared])  56.8 us
    all_gather x2, blocking collectives, carried_in(): pieces = jax.tree.map(lambda part: lax.all_gather(part, axis), value)  52.6 us
  transfers between devices with their start and end apart: 15, of which 15 were waited for; matrix products, arithmetic and copies ran while one was open for 10% of the time, Pallas kernels for 0%

commit v1 on v0

v1 whole, which is shorter than its diff:
```python
import functools
import math

import jax
import jax.numpy as jnp
from jax import lax
from jax.experimental import pallas as pl
from jax.experimental.pallas import tpu as pltpu
from jax.sharding import PartitionSpec as P

FINE = 2
NEWTON = 2
SHIFT = 8.0
LANES = 128
MESH = pl.DeviceIdType.MESH
F32 = jnp.float32
BF16 = jnp.bfloat16

COL_MASS, COL_SIN, COL_GAIN, COL_SHARED, COL_NODE, COL_LINK, COL_COND = 0, 16, 48, 64, 72, 80, 88
FLOW_G, FLOW_P, BACK_P, BACK_Q, SETUP, GRAM, LAST = range(7)


def halves(acc):
    return acc[:, :LANES] + acc[:, LANES:]


def split(value):
    high = value.astype(BF16)
    low = (value - high.astype(F32)).astype(BF16)
    return jnp.concatenate([high, low], axis=1)


def dot(a, b):
    return jnp.dot(a, b, preferred_element_type=F32)


def ones_where(mask):
    return jnp.where(mask, 1.0, 0.0).astype(BF16)


def kernel(
    cap,
    width,
    n_tm,
    n_dom,
    x0_ref,
    w0_ref,
    gain_in_ref,
    gain_sh_ref,
    jac_ref,
    off_ref,
    block_link_ref,
    mass_ref,
    shared_mass_ref,
    shared_diag_ref,
    node_ref,
    link_ref,
    link_smem,
    cond_ref,
    amp_ref,
    phase_ref,
    nonlin_ref,
    out_in_ref,
    out_sh_ref,
    flag_ref,
    x,
    jx,
    g,
    p,
    q,
    fixed,
    flow,
    g_parts,
    p_parts,
    flow_parts,
    slot_parts,
    blocks,
    node_rows,
    node_cols,
    pack,
    unpack,
    own,
    own_t,
    table,
    table_t,
    table2_t,
    link_mass,
    link_cond,
    diag_sh,
    stage,
    recv,
    set_send,
    set_recv,
    gain_send,
    gain_recv,
    gram_send,
    gram_recv,
    jump_send,
    jump_recv,
    value_send,
    value_sh,
    send_sem,
    recv_sem,
    tm_send,
    tm_recv,
):
    me_t, me_d = lax.axis_index("tm"), lax.axis_index("dom")
    nodes = x0_ref.shape[0]
    shard = w0_ref.shape[0] // n_dom
    links = flow.shape[0]
    chunks, shard_chunks, link_chunks = nodes // LANES, shard // LANES, links // LANES
    at_sh, at_link = nodes, nodes + shard
    per_owner = width // LANES
    nblocks, bsize = jac_ref.shape[0], jac_ref.shape[1]
    iota0 = lax.broadcasted_iota(jnp.int32, (LANES, LANES), 0)
    iota1 = lax.broadcasted_iota(jnp.int32, (LANES, LANES), 1)

    def rows(start, size):
        return pl.ds(pl.multiple_of(start, size), size)

    def dom_peer(step):
        return lax.rem(me_d + step, n_dom)

    def dom_source(step):
        return lax.rem(me_d + n_dom - step, n_dom)

    def tm_peer(step):
        return lax.rem(me_t + step, n_tm)

    def tm_source(step):
        return lax.rem(me_t + n_tm - step, n_tm)

    def dom_copy(kind, step, source, target):
        return pltpu.make_async_remote_copy(
            src_ref=source,
            dst_ref=target,
            send_sem=send_sem.at[kind, step],
            recv_sem=recv_sem.at[kind, step],
            device_id={"dom": dom_peer(step)},
            device_id_type=MESH,
        )

    def tm_copy(kind, step, source, target):
        return pltpu.make_async_remote_copy(
            src_ref=source,
            dst_ref=target,
            send_sem=tm_send.at[kind, step],
            recv_sem=tm_recv.at[kind, step],
            device_id={"tm": tm_peer(step)},
            device_id_type=MESH,
        )

    if cap < width:
        for kind in range(4):
            for o in range(n_dom):
                recv[kind, o, cap:, :] = jnp.zeros((width - cap, LANES), F32)
    barrier = pltpu.get_barrier_semaphore()
    for step in range(1, n_dom):
        pl.semaphore_signal(barrier, inc=1, device_id={"dom": dom_peer(step)}, device_id_type=MESH)
    for step in range(1, n_tm):
        pl.semaphore_signal(barrier, inc=1, device_id={"tm": tm_peer(step)}, device_id_type=MESH)

    slice_f = me_t.astype(F32)
    table[...] = jnp.zeros((LANES, LANES), F32)
    table[COL_MASS : COL_MASS + chunks, :] = mass_ref[...]
    for k in range(FINE):
        angle = (slice_f * FINE + (k + 1.0)) * (2.0 * math.pi / (n_tm * FINE))
        at = COL_SIN + chunks * k
        table[at : at + chunks, :] = jnp.sin(angle + phase_ref[...])
    table[COL_GAIN : COL_GAIN + chunks, :] = gain_in_ref[...]
    for a in range(shard_chunks):
        row = shard_chunks * me_d + a
        table[COL_SHARED + a : COL_SHARED + a + 1, :] = shared_mass_ref[pl.ds(row, 1), :]
        table[COL_SHARED + 2 + a : COL_SHARED + 3 + a, :] = shared_diag_ref[pl.ds(row, 1), :]
        table[COL_SHARED + 4 + a : COL_SHARED + 5 + a, :] = gain_sh_ref[pl.ds(row, 1), :]
    table[COL_NODE : COL_NODE + link_chunks, :] = node_ref[...].astype(F32)
    table[COL_LINK : COL_LINK + link_chunks, :] = link_ref[...].astype(F32)
    table[COL_COND : COL_COND + link_chunks, :] = cond_ref[...]
    table_t[...] = table[...].T

    def column(at):
        return table_t[:, at : at + 1]

    link_col = [column(COL_LINK + j).astype(jnp.int32) for j in range(link_chunks)]
    link_row = [link_ref[j : j + 1, :] for j in range(link_chunks)]
    if cap == width:
        slot_col, slot_row = link_col, link_row
        crowd = jnp.zeros((1, LANES), F32)
    else:
        owner_col = [v // shard for v in link_col]
        owner_row = [v // shard for v in link_row]
        slot_col, slot_row = [], []
        crowd = jnp.zeros((1, LANES), F32)
        for j in range(link_chunks):
            rank_row = jnp.zeros((1, LANES), F32)
            rank_col = jnp.zeros((LANES, 1), F32)
            for i in range(j + 1):
                same_row = owner_col[i] == owner_row[j]
                same_col = owner_col[j] == owner_row[i]
                if i == j:
                    same_row = same_row & (iota0 < iota1)
                    same_col = same_col & (iota1 < iota0)
                rank_row += jnp.sum(jnp.where(same_row, 1.0, 0.0), axis=0, keepdims=True)
                rank_col += jnp.sum(jnp.where(same_col, 1.0, 0.0), axis=1, keepdims=True)
            crowd = jnp.maximum(crowd, rank_row)
            slot_row.append(owner_row[j] * width + rank_row.astype(jnp.int32))
            slot_col.append(owner_col[j] * width + rank_col.astype(jnp.int32))
    set_send[...] = jnp.zeros(set_send.shape, F32)
    for i in range(n_dom * per_owner):
        held = jnp.full((1, LANES), -1.0, F32)
        total = jnp.zeros((1, LANES), F32)
        for j in range(link_chunks):
            here = (iota1 + LANES * i) == slot_col[j]
            local = (link_col[j] % shard).astype(F32)
            held = jnp.maximum(held, jnp.max(jnp.where(here, local, -1.0), axis=0, keepdims=True))
            total += jnp.sum(jnp.where(here, column(COL_COND + j), 0.0), axis=0, keepdims=True)
            unpack[LANES * j : LANES * (j + 1), LANES * i : LANES * (i + 1)] = ones_where(here)
            pack[LANES * i : LANES * (i + 1), LANES * j : LANES * (j + 1)] = ones_where(
                (iota0 + LANES * i) == slot_row[j]
            )
        o, h = i // per_owner, i % per_owner
        set_send[o, h : h + 1, :] = held
        set_send[o, 2 + h : 3 + h, :] = total
    for o in range(n_dom):
        set_send[o, 4:5, :] = crowd
    gain_send[...] = jnp.zeros(gain_send.shape, F32)
    for m in range(n_tm):
        gain_send[m, 0:1, :] = gain_in_ref[m : m + 1, :]
        row = shard_chunks * me_d + m * shard_chunks // n_tm
        gain_send[m, 1:2, :] = gain_sh_ref[pl.ds(row, 1), :]

    pl.semaphore_wait(barrier, n_dom - 1 + n_tm - 1)
    for step in range(1, n_dom):
        dom_copy(SETUP, step, set_send.at[dom_peer(step)], set_recv.at[me_d]).start()
    for step in range(1, n_tm):
        tm_copy(0, step, gain_send.at[tm_peer(step)], gain_recv.at[me_t]).start()
    set_recv[me_d] = set_send[me_d]
    gain_recv[me_t] = gain_send[me_t]

    for j in range(link_chunks):
        node_row = node_ref[j : j + 1, :]
        node_col = column(COL_NODE + j).astype(jnp.int32)
        link_cond[LANES * j : LANES * (j + 1), :] = jnp.broadcast_to(column(COL_COND + j), (LANES, LANES))
        across = slice(LANES * j, LANES * (j + 1))

        def select(i, carry):
            base = pl.multiple_of(i * LANES, LANES)
            node_rows[pl.ds(base, LANES), across] = ones_where(iota0 + base == node_row)
            node_cols[across, pl.ds(base, LANES)] = ones_where(iota1 + base == node_col)
            return carry

        lax.fori_loop(0, chunks, select, 0, unroll=2)
        mass_sum = jnp.zeros((LANES, LANES), F32)
        for i in range(w0_ref.shape[0] // LANES):
            mass_sum += jnp.where(iota1 + LANES * i == link_col[j], shared_mass_ref[i : i + 1, :], 0.0)
        link_mass[across, :] = jnp.broadcast_to(jnp.sum(mass_sum, axis=1, keepdims=True), (LANES, LANES))

    def cut(b, carry):
        blocks[b] = split(jnp.concatenate([jac_ref[b], off_ref[b]], axis=1))
        return carry

    lax.fori_loop(0, nblocks, cut, 0, unroll=2)

    each = LANES // bsize

    def begin(i, carry):
        at = rows(i * LANES, LANES)
        value = x0_ref[at, :]
        x[at, :] = value
        g_parts[pl.ds(i * each, each)] = split(value).reshape(each, bsize, 2 * LANES)
        return carry

    lax.fori_loop(0, chunks, begin, 0)
    x[at_sh : at_sh + shard, :] = w0_ref[rows(me_d * shard, shard), :]

    def fetch(l, carry):
        x[pl.ds(at_link + l, 1), :] = w0_ref[pl.ds(link_smem[l // LANES, lax.rem(l, LANES)], 1), :]
        return carry

    lax.fori_loop(0, links, fetch, 0, unroll=8)

    for step in range(1, n_dom):
        dom_copy(SETUP, step, set_send.at[dom_peer(step)], set_recv.at[dom_source(step)]).wait_recv()
    for o in range(n_dom):
        for h in range(per_owner):
            at = o * per_owner + h
            table[at : at + 1, :] = set_recv[o, h : h + 1, :]
    table2_t[...] = table[...].T
    sums = [jnp.zeros((LANES, LANES), F32) for a in range(shard_chunks)]
    crowd = jnp.zeros((1, LANES), F32)
    for o in range(n_dom):
        crowd = jnp.maximum(crowd, set_recv[o, 4:5, :])
        for h in range(per_owner):
            i = o * per_owner + h
            held_row = set_recv[o, h : h + 1, :].astype(jnp.int32)
            held_col = table2_t[:, i : i + 1].astype(jnp.int32)
            for a in range(shard_chunks):
                here = (iota0 + LANES * a) == held_row
                sums[a] += jnp.where(here, set_recv[o, 2 + h : 3 + h, :], 0.0)
                own[LANES * a : LANES * (a + 1), LANES * i : LANES * (i + 1)] = ones_where(here)
                own_t[LANES * i : LANES * (i + 1), LANES * a : LANES * (a + 1)] = ones_where(
                    (iota1 + LANES * a) == held_col
                )
    for a in range(shard_chunks):
        total = column(COL_SHARED + 2 + a) + jnp.sum(sums[a], axis=1, keepdims=True)
        diag_sh[LANES * a : LANES * (a + 1), :] = jnp.broadcast_to(total, (LANES, LANES))
    flag_ref[...] = jnp.broadcast_to(crowd, flag_ref.shape)

    def apply_blocks(parts, out):
        def one(b, carry):
            other = block_link_ref[b]
            mine, theirs = parts[b], parts[other]
            acc = dot(blocks[b], jnp.concatenate([mine, theirs, mine, theirs], axis=0))
            out[rows(b * bsize, bsize), :] = halves(acc)
            return carry

        lax.fori_loop(0, nblocks, one, 0, unroll=4)

    def gather_flow(parts):
        flow[...] = halves(dot(node_cols[...], parts[...].reshape(nodes, 2 * LANES))) * link_cond[...]

    def add_flow(vec, out, shift_by=None, parts=None):
        flow_parts[...] = split(flow[...] - link_cond[...] * vec[at_link : at_link + links, :])
        size = 2 * LANES

        def one(i, carry):
            at = rows(i * size, size)
            value = out[at, :] + halves(dot(node_rows[at, :], flow_parts[...]))
            if shift_by is not None:
                value = value - SHIFT * shift_by[at, :]
            out[at, :] = value
            if parts is not None:
                parts[pl.ds(i * 2 * each, 2 * each)] = split(value).reshape(2 * each, bsize, 2 * LANES)
            return carry

        lax.fori_loop(0, nodes // size, one, 0)

    def start_exchange(kind):
        for step in range(1, n_dom):
            dom_copy(
                kind,
                step,
                stage.at[kind, dom_peer(step), pl.ds(0, cap)],
                recv.at[kind, me_d, pl.ds(0, cap)],
            ).start()
        recv[kind, me_d] = stage[kind, me_d]

    def wait_exchange(kind, receive):
        for step in range(1, n_dom):
            copy = dom_copy(
                kind,
                step,
                stage.at[kind, dom_peer(step), pl.ds(0, cap)],
                recv.at[kind, dom_source(step), pl.ds(0, cap)],
            )
            if receive:
                copy.wait_recv()
            else:
                copy.wait_send()

    def send_flow(kind):
        flow_parts[...] = split(flow[...])

        def one(o, carry):
            stage[kind, o] = halves(dot(pack[rows(o * width, width), :], flow_parts[...]))
            return carry

        lax.fori_loop(0, n_dom, one, 0)
        start_exchange(kind)

    def load_slots(kind):
        for o in range(n_dom):
            slot_parts[o * width : (o + 1) * width, :] = split(recv[kind, o])

    def collect_flow(kind):
        wait_exchange(kind, True)
        load_slots(kind)
        return halves(dot(own[...], slot_parts[...]))

    def send_back(kind, value):
        value_parts = split(value)

        def one(o, carry):
            stage[kind, o] = halves(dot(own_t[rows(o * width, width), :], value_parts))
            return carry

        lax.fori_loop(0, n_dom, one, 0)
        start_exchange(kind)

    def take_back(kind, out):
        wait_exchange(kind, True)
        load_slots(kind)
        out[at_link : at_link + links, :] = halves(dot(unpack[...], slot_parts[...]))

    def set_fixed(k):
        for i in range(chunks):
            at = slice(LANES * i, LANES * (i + 1))
            drive = amp_ref[at, :] * column(COL_SIN + chunks * k + i)
            fixed[at, :] = column(COL_MASS + i) * x[at, :] + drive
        for a in range(shard_chunks):
            at = slice(at_sh + LANES * a, at_sh + LANES * (a + 1))
            fixed[at, :] = column(COL_SHARED + a) * x[at, :]
        fixed[at_link:, :] = link_mass[...] * x[at_link:, :]

    def new_residual():
        def one(i, carry):
            at = rows(i * LANES, LANES)
            value = fixed[at, :] - jx[at, :] - nonlin_ref[...] * jnp.tanh(x[at, :])
            g[at, :] = value
            g_parts[pl.ds(i * each, each)] = split(value).reshape(each, bsize, 2 * LANES)
            return carry

        lax.fori_loop(0, chunks, one, 0)
        g[nodes:, :] = fixed[nodes:, :] - jx[nodes:, :]

    gather_flow(g_parts)
    send_flow(FLOW_G)
    apply_blocks(g_parts, jx)
    add_flow(x, jx)
    set_fixed(0)
    at = slice(at_sh, at_sh + shard)
    wait_exchange(FLOW_G, False)
    jx[at, :] = diag_sh[...] * x[at, :] - collect_flow(FLOW_G)
    send_back(BACK_P, jx[at, :])
    take_back(BACK_P, jx)
    wait_exchange(BACK_P, False)
    new_residual()

    def gram_row(index, total):
        return total[index : index + 1, :]

    def newton(turn, carry):
        gather_flow(g_parts)
        send_flow(FLOW_G)
        apply_blocks(g_parts, p)
        add_flow(g, p, g, p_parts)
        gather_flow(p_parts)
        send_flow(FLOW_P)
        apply_blocks(p_parts, q)
        p[at, :] = (diag_sh[...] - SHIFT) * g[at, :] - collect_flow(FLOW_G)
        send_back(BACK_P, p[at, :])
        q[at, :] = diag_sh[...] * p[at, :] - collect_flow(FLOW_P)
        send_back(BACK_Q, q[at, :])
        take_back(BACK_P, p)
        add_flow(p, q)

        def gram(i, sums):
            here = rows(i * LANES, LANES)
            vg, vp, vq = g[here, :], p[here, :], q[here, :]
            pairs = ((vg, vg), (vg, vp), (vp, vp), (vg, vq), (vp, vq), (vq, vq))
            return tuple(
                s + jnp.sum((a * b).reshape(LANES // 8, 8, LANES), axis=0)
                for s, (a, b) in zip(sums, pairs)
            )

        zero = jnp.zeros((8, LANES), F32)
        sums = lax.fori_loop(0, chunks + shard_chunks, gram, (zero,) * 6)
        for i, s in enumerate(sums):
            gram_send[i : i + 1, :] = jnp.sum(s, axis=0, keepdims=True)
        gram_send[6:8, :] = jnp.zeros((2, LANES), F32)
        for step in range(1, n_dom):
            dom_copy(GRAM, step, gram_send, gram_recv.at[me_d]).start()
        gram_recv[me_d] = gram_send[...]
        for kind in (FLOW_G, FLOW_P, BACK_P, BACK_Q):
            wait_exchange(kind, False)
        for step in range(1, n_dom):
            copy = dom_copy(GRAM, step, gram_send, gram_recv.at[dom_source(step)])
            copy.wait_send()
            copy.wait_recv()
        total = gram_recv[0]
        for o in range(1, n_dom):
            total = total + gram_recv[o]
        gg, gp, pp, gq, pq, qq = [total[i : i + 1, :] for i in range(6)]
        norm2 = gg + 1e-30
        inv2 = 1.0 / norm2
        h00 = (gp + SHIFT * gg) * inv2
        turnover = h00 - SHIFT
        tail2 = pp - 2.0 * turnover * gp + turnover * turnover * gg
        inv_both = 1.0 / (jnp.sqrt(norm2) * jnp.sqrt(tail2))
        inv_tail2 = 1.0 / tail2
        push = turnover * SHIFT
        g_s = gq - turnover * gp - push * gg
        p_s = pq - turnover * pp - push * gp
        q_s = qq - turnover * pq - push * gq
        t_s = p_s - turnover * g_s
        s_s = q_s - turnover * p_s - push * g_s
        g_t = gp - turnover * gg
        h10 = tail2 * inv_both
        h01 = g_s * inv_both
        h11 = t_s * inv_tail2
        h21_2 = (
            s_s * inv_tail2
            - h01 * h01 * (2.0 - gg * inv2)
            - h11 * h11
            + 2.0 * h01 * h11 * g_t * inv_both
        )
        n11 = h00 * h00 + h10 * h10
        n12 = h00 * h01 + h10 * h11
        n22 = h01 * h01 + h11 * h11 + h21_2
        inv_det = 1.0 / (n11 * n22 - n12 * n12)
        c_p = norm2 * inv_both * (h01 * n11 - h00 * n12) * inv_det
        c_g = (h00 * n22 - h01 * n12) * inv_det - turnover * c_p

        def advance(here):
            vg, vp = g[here, :], p[here, :]
            x[here, :] = x[here, :] + c_g * vg + c_p * vp
            jx[here, :] = jx[here, :] + c_g * (vp + SHIFT * vg) + c_p * q[here, :]

        def one(i, carry):
            advance(rows(i * LANES, LANES))
            return carry

        lax.fori_loop(0, chunks + shard_chunks, one, 0)
        take_back(BACK_Q, q)
        advance(slice(at_link, at_link + links))

        @pl.when(turn == NEWTON - 1)
        def _():
            set_fixed(1)

        @pl.when(turn < FINE * NEWTON - 1)
        def _():
            new_residual()

        return carry

    lax.fori_loop(0, FINE * NEWTON, newton, 0)

    per_rows, per_shared = nodes // n_tm, shard // n_tm
    for i in range(chunks):
        here = slice(LANES * i, LANES * (i + 1))
        jump_send[i, :per_rows, :] = x[here, :] - column(COL_GAIN + i) * x0_ref[here, :]
    for a in range(shard_chunks):
        here = slice(at_sh + LANES * a, at_sh + LANES * (a + 1))
        start = w0_ref[rows(me_d * shard + LANES * a, LANES), :]
        jump = x[here, :] - column(COL_SHARED + 4 + a) * start
        pieces = LANES // per_shared
        for m in range(pieces):
            jump_send[a * pieces + m, per_rows:, :] = jump[per_shared * m : per_shared * (m + 1), :]
    for step in range(1, n_tm):
        tm_copy(1, step, jump_send.at[tm_peer(step)], jump_recv.at[me_t]).start()
    jump_recv[me_t] = jump_send[me_t]
    for step in range(1, n_tm):
        tm_copy(0, step, gain_send.at[tm_peer(step)], gain_recv.at[tm_source(step)]).wait_recv()
    for m in range(n_tm):
        table[m : m + 1, :] = gain_recv[m, 0:1, :]
        table[n_tm + m : n_tm + m + 1, :] = gain_recv[m, 1:2, :]
    table2_t[...] = table[...].T
    my_shared = rows(lax.rem(me_t, LANES // per_shared) * per_shared, per_shared)
    for step in range(1, n_tm):
        tm_copy(1, step, jump_send.at[tm_peer(step)], jump_recv.at[tm_source(step)]).wait_recv()
    for part, gains in (
        (slice(0, per_rows), [table2_t[:, m : m + 1] for m in range(n_tm)]),
        (
            slice(per_rows, per_rows + per_shared),
            [table2_t[my_shared, n_tm + m : n_tm + m + 1] for m in range(n_tm)],
        ),
    ):
        whole, total = gains[0], jump_recv[0, part, :]
        for m in range(1, n_tm):
            whole = whole * gains[m]
            total = gains[m] * total + jump_recv[m, part, :]
        value = total / (1.0 - whole)
        for m in range(n_tm):
            value_send[m, part, :] = value
            if m + 1 < n_tm:
                value = gains[m] * value + jump_recv[m, part, :]

    def value_copy(step, holder):
        source = value_send.at[tm_peer(step), pl.ds(0, per_rows)]
        return tm_copy(2, step, source, out_in_ref.at[rows(holder * per_rows, per_rows)])

    def shared_copy(step, holder):
        source = value_send.at[tm_peer(step), pl.ds(per_rows, per_shared)]
        return tm_copy(3, step, source, value_sh.at[rows(holder * per_shared, per_shared)])

    for step in range(1, n_tm):
        shared_copy(step, me_t).start()
        value_copy(step, me_t).start()
    out_in_ref[rows(me_t * per_rows, per_rows), :] = value_send[me_t, :per_rows, :]
    value_sh[rows(me_t * per_shared, per_shared), :] = value_send[me_t, per_rows:, :]
    for step in range(1, n_tm):
        shared_copy(step, tm_source(step)).wait_recv()
    for step in range(1, n_dom):
        dom_copy(LAST, step, value_sh, out_sh_ref.at[rows(me_d * shard, shard)]).start()
    out_sh_ref[rows(me_d * shard, shard), :] = value_sh[...]
    for step in range(1, n_tm):
        value_copy(step, tm_source(step)).wait_recv()
    for step in range(1, n_dom):
        copy = dom_copy(LAST, step, value_sh, out_sh_ref.at[rows(dom_source(step) * shard, shard)])
        copy.wait_recv()
        copy.wait_send()
        dom_copy(SETUP, step, set_send.at[dom_peer(step)], set_recv.at[me_d]).wait_send()
    for step in range(1, n_tm):
        tm_copy(0, step, gain_send.at[tm_peer(step)], gain_recv.at[me_t]).wait_send()
        tm_copy(1, step, jump_send.at[tm_peer(step)], jump_recv.at[me_t]).wait_send()
        shared_copy(step, me_t).wait_send()
        value_copy(step, me_t).wait_send()


def run(cap, width, collective_id, n_tm, n_dom, operands):
    nodes, samples = operands[0].shape
    shared = operands[1].shape[0]
    shard = shared // n_dom
    links = operands[10].shape[0] * operands[10].shape[1]
    nblocks, bsize = operands[4].shape[0], operands[4].shape[1]
    total = nodes + shard + links
    slots = n_dom * width
    piece = (nodes + shard) // n_tm
    vmem = pl.BlockSpec(memory_space=pltpu.VMEM)
    smem = pl.BlockSpec(memory_space=pltpu.SMEM)
    specs = [vmem] * len(operands)
    specs[6] = smem
    specs[12] = smem
    state = pltpu.VMEM((total, samples), F32)
    tile = pltpu.VMEM((LANES, LANES), F32)
    return pl.pallas_call(
        functools.partial(kernel, cap, width, n_tm, n_dom),
        out_shape=(
            jax.ShapeDtypeStruct((nodes, samples), F32),
            jax.ShapeDtypeStruct((shared, samples), F32),
            jax.ShapeDtypeStruct((8, LANES), F32),
        ),
        in_specs=specs,
        out_specs=(vmem, vmem, vmem),
        scratch_shapes=[
            state,
            state,
            state,
            state,
            state,
            state,
            pltpu.VMEM((links, samples), F32),
            pltpu.VMEM((nblocks, bsize, 2 * samples), BF16),
            pltpu.VMEM((nblocks, bsize, 2 * samples), BF16),
            pltpu.VMEM((links, 2 * samples), BF16),
            pltpu.VMEM((slots, 2 * samples), BF16),
            pltpu.VMEM((nblocks, bsize, 4 * bsize), BF16),
            pltpu.VMEM((nodes, links), BF16),
            pltpu.VMEM((links, nodes), BF16),
            pltpu.VMEM((slots, links), BF16),
            pltpu.VMEM((links, slots), BF16),
            pltpu.VMEM((shard, slots), BF16),
            pltpu.VMEM((slots, shard), BF16),
            tile,
            tile,
            tile,
            pltpu.VMEM((links, samples), F32),
            pltpu.VMEM((links, samples), F32),
            pltpu.VMEM((shard, samples), F32),
            pltpu.VMEM((4, n_dom, width, samples), F32),
            pltpu.VMEM((4, n_dom, width, samples), F32),
            pltpu.VMEM((n_dom, 8, LANES), F32),
            pltpu.VMEM((n_dom, 8, LANES), F32),
            pltpu.VMEM((n_tm, 8, LANES), F32),
            pltpu.VMEM((n_tm, 8, LANES), F32),
            pltpu.VMEM((8, LANES), F32),
            pltpu.VMEM((n_dom, 8, LANES), F32),
            pltpu.VMEM((n_tm, piece, samples), F32),
            pltpu.VMEM((n_tm, piece, samples), F32),
            pltpu.VMEM((n_tm, piece, samples), F32),
            pltpu.VMEM((shard, samples), F32),
            pltpu.SemaphoreType.DMA((7, n_dom)),
            pltpu.SemaphoreType.DMA((7, n_dom)),
            pltpu.SemaphoreType.DMA((4, n_tm)),
            pltpu.SemaphoreType.DMA((4, n_tm)),
        ],
        compiler_params=pltpu.CompilerParams(
            collective_id=collective_id, has_side_effects=True, vmem_limit_bytes=62 * 1024 * 1024
        ),
        name="parareal",
    )(*operands)


def shards(
    state_interior,
    state_shared,
    gain_interior,
    gain_shared,
    jac_blocks,
    off_blocks,
    block_link,
    mass,
    shared_mass,
    shared_diag,
    link_node,
    link_shared,
    link_cond,
    source_amp,
    phase,
    nonlin,
):
    n_tm, n_dom = lax.axis_size("tm"), lax.axis_size("dom")

    def lanes(value):
        return value.reshape(-1, LANES)

    operands = (
        state_interior[0],
        state_shared[0],
        lanes(gain_interior),
        lanes(gain_shared),
        jac_blocks,
        off_blocks,
        block_link,
        lanes(mass),
        lanes(shared_mass),
        lanes(shared_diag),
        lanes(link_node),
        lanes(link_shared),
        lanes(link_shared),
        lanes(link_cond),
        source_amp,
        lanes(phase),
        lanes(nonlin),
    )
    shard = state_shared.shape[1] // n_dom
    new_in, new_sh, crowd = run(shard, shard, 0, n_tm, n_dom, operands)
    return (new_in[None], new_sh[None])


def solution(mesh):
    return jax.shard_map(
        shards,
        mesh=mesh,
        in_specs=(
            P("tm", "dom", None),
            P("tm", None, None),
            P("tm", "dom"),
            P("tm", None),
            P("dom", None, None),
            P("dom", None, None),
            P("dom"),
            P("dom"),
            P(),
            P(),
            P("dom"),
            P("dom"),
            P("dom"),
            P("dom", None),
            P("dom"),
            P(),
        ),
        out_specs=(P("tm", "dom", None), P("tm", None, None)),
        check_vma=False,
    )
```

time: 1780 us -> 320 us (0.18)
  waiting for transfers between devices: 892 us -> 0 us
  blocking collectives: 406 us -> 0 us
  Pallas kernels: 0 us -> 315 us
  other arithmetic: 298 us -> 0 us
  local copies, waits for them, and re-layouts: 85.5 us -> 3.32 us
  matrix products: 63 us -> 0 us
    psum x13 -> x0, waiting for transfers between devices: 716 us -> none  [the longest x12 634 us: operate_on(): out_sh = lax.psum(partial_flow, 'dom') + shared_diag[:, None] * vec_sh]
    psum x21 -> x0, blocking collectives: 353 us -> none  [the longest x20 294 us: inner_sums(): return lax.psum(part_in, 'dom') + part_sh]
    pallas_call x0 -> x1, Pallas kernels: none -> 315 us  [run(): pl.pallas_call(functools.partial(kernel, cap, width, n_tm, n_dom), out_sh...]
    all_gather x2 -> x0, waiting for transfers between devices: 175 us -> none  [carried_in(): pieces = jax.tree.map(lambda part: lax.all_gather(part, axis), value)]
    scatter-add x24 -> x0, other arithmetic: 113 us -> none  [the longest x12 68.6 us: operate_local(): out_in = out_in.at[link_node].add(link_flow)]
    gather x36 -> x0, local copies, waits for them, and re-layouts: 84.9 us -> none  [the longest x24 56.8 us: operate_local(): link_flow = link_cond[:, None] * (vec_in[link_node] - vec_sh[link_shared])]
    reduce_sum x32 -> x0, other arithmetic: 69 us -> none  [the longest x20 46.2 us: inner_sums(): part_sh = jnp.stack([jnp.sum(v * other_sh, axis=0) for v in vecs_sh])]
    dot_general x24 -> x0, matrix products: 63 us -> none  [the longest x12 37 us: operate_local(): jnp.einsum('bij,bjs->bis', off_blocks, blocked[block_link], precision=hig...]
  transfers between devices with their start and end apart: 15 -> 0, of which waited for: 15 -> 0; matrix products, arithmetic and copies ran while one was open for 10% -> 0% of each run, Pallas kernels for 0% -> 0%
where the time goes in v1:
time: 320 us; the launch traced here: 319 us
  Pallas kernels  315 us (98%)
  local copies, waits for them, and re-layouts  3.32 us (1%)
    pallas_call x1, Pallas kernels, run(): pl.pallas_call(functools.partial(kernel, cap, width, n_tm, n_dom), out_sh...  315 us

profile of v1, /device:TPU:1, one launch (start us, length us, event | category | flops | bytes accessed | tf_op | source)
XLA Modules:
  0.0 319.2 jit_solution(10187506397559888682)
XLA Ops:
  0.6 315.2 %parareal.1 = (f32[2048,128]{1,0:T(8,128)}, f32[2048,128]{1,0:T(8,128)}, f32[8,128]{1,0:T(8,128)}) custom-call(f32[2048,128]{1,0:T(8,128)} %bitcast.16, f32[2048,128]{1,0:T(8,128)} %bitcast.17, f32[16,128]{1,0:T(8,128)} %bitcast.18, f32[16,128]{1,0:T(8,128)} %bitcast.19, f32[32,64,64]{2,1,0:T(8,128)} %jac_ref.1, f32[32,64,64]{2,1,0:T(8,128)} %off_ref.1, ...), custom_call_target="tpu_custom_call" | custom-call | tf_op jit(solution)/shard_map/parareal/pallas_call | solution.py:617
  315.9 0.0 copy-start
  315.9 2.4 copy.20
  318.2 0.0 copy-done
  318.2 1.0 copy.21
Async XLA Ops:
  315.9 2.4 copy-start

commit v2 on v1

--- a/solution.py
+++ b/solution.py
@@ -11,6 +11,7 @@
 FINE = 2
 NEWTON = 2
 SHIFT = 8.0
+SLOTS = 96
 LANES = 128
 MESH = pl.DeviceIdType.MESH
 F32 = jnp.float32
@@ -715,7 +716,12 @@
         lanes(nonlin),
     )
     shard = state_shared.shape[1] // n_dom
-    new_in, new_sh, crowd = run(shard, shard, 0, n_tm, n_dom, operands)
+    new_in, new_sh, crowd = run(SLOTS, LANES, 0, n_tm, n_dom, operands)
+    new_in, new_sh = lax.cond(
+        jnp.max(crowd) < SLOTS,
+        lambda: (new_in, new_sh),
+        lambda: run(shard, shard, 1, n_tm, n_dom, operands)[:2],
+    )
     return (new_in[None], new_sh[None])
 
 

time: 320 us -> 204 us (0.64)
  Pallas kernels: 315 us -> 196 us
    pallas_call x1, Pallas kernels: 315 us -> 196 us  [run(): pl.pallas_call(functools.partial(kernel, cap, width, n_tm, n_dom), out_sh...]
where the time goes in v2:
time: 204 us
  Pallas kernels  196 us (96%)
  local copies, waits for them, and re-layouts  4.63 us (2%)
    pallas_call x1, Pallas kernels, run(): pl.pallas_call(functools.partial(kernel, cap, width, n_tm, n_dom), out_sh...  196 us
    unnamed x28, local copies, waits for them, and re-layouts  4.63 us

profile of v2, /device:TPU:1, one launch (start us, length us, event | category | flops | bytes accessed | tf_op | source)
XLA Modules:
  0.0 203.7 jit_solution(5625645543075850493)
XLA Ops:
  0.6 0.0 copy-start.4
  0.6 0.0 copy-start.3
  0.7 0.0 copy-start.2
  0.7 0.0 copy-start.11
  0.7 0.7 copy-done.4
  1.3 0.0 copy-done.3
  1.3 0.0 copy-done.2
  1.4 0.0 copy-done.11
  1.4 0.0 copy-start
  1.4 0.0 copy-start.6
  1.4 0.0 copy-start.7
  1.4 0.0 copy-start.9
  1.4 0.0 copy-start.10
  1.4 196.4 %parareal.3 = (f32[2048,128]{1,0:T(8,128)}, f32[2048,128]{1,0:T(8,128)}, f32[8,128]{1,0:T(8,128)}) custom-call(f32[2048,128]{1,0:T(8,128)} %bitcast.14, f32[2048,128]{1,0:T(8,128)} %bitcast.16, f32[16,128]{1,0:T(8,128)S(1)} %bitcast.20, f32[16,128]{1,0:T(8,128)S(1)} %bitcast.22, f32[32,64,64]{2,1,0:T(8,128)} %jac_ref.1, f32[32,64,64]{2,1,0:T(8,128)} %off_ref.1, ...), custom_call_target="tpu_custom_call" | custom-call | tf_op jit(solution)/shard_map/parareal/pallas_call | solution.py:618
  197.8 0.0 copy-start.5
  197.8 1.3 reduce_max.9
  199.1 0.0 copy-start.8
  199.7 0.0 copy-start.12
  199.8 0.0 copy-done
  199.8 0.0 copy-done.6
  199.8 0.0 copy-done.7
  199.8 0.0 copy-done.9
  199.8 0.0 copy-done.10
  199.8 0.0 copy-done.5
  199.8 0.0 copy-done.8
  199.8 0.6 copy-done.12
  200.4 0.0 copy-start.1
  200.4 2.4 %copy.24 = f32[1,2048,128]{2,1,0:T(8,128)} copy(f32[1,2048,128]{2,1,0:T(8,128)} %bitcast.18) | data formatting | bytes 2097152
  202.8 0.0 copy-done.1
  202.8 1.0 copy.25
  (1 shorter events, 0.0 us)
Async XLA Ops:
  0.6 0.7 copy-start.4
  0.6 0.7 copy-start.3
  0.7 0.7 copy-start.2
  0.7 0.7 copy-start.11
  1.4 198.4 %copy-start = (f32[1,2048,128]{2,1,0:T(8,128)S(1)}, f32[1,2048,128]{2,1,0:T(8,128)}, u32[]{:S(2)}) copy-start(f32[1,2048,128]{2,1,0:T(8,128)} %param.18) | copy-start | bytes 3145732
  1.4 198.4 %copy-start.6 = (f32[2048]{0:T(1024)S(1)}, f32[2048]{0:T(1024)}, u32[]{:S(2)}) copy-start(f32[2048]{0:T(1024)} %param.27) | copy-start | bytes 24580
  1.4 198.4 %copy-start.7 = (f32[2048]{0:T(1024)S(1)}, f32[2048]{0:T(1024)}, u32[]{:S(2)}) copy-start(f32[2048]{0:T(1024)} %param.32) | copy-start | bytes 24580
  1.4 198.4 %copy-start.9 = (s32[512]{0:T(512)S(1)}, s32[512]{0:T(512)}, u32[]{:S(2)}) copy-start(s32[512]{0:T(512)} %param.28) | copy-start | bytes 6148
  1.4 198.4 %copy-start.10 = (f32[512]{0:T(512)S(1)}, f32[512]{0:T(512)}, u32[]{:S(2)}) copy-start(f32[512]{0:T(512)} %param.30) | copy-start | bytes 6148
  197.8 2.0 %copy-start.5 = (f32[2048]{0:T(1024)S(1)}, f32[2048]{0:T(1024)}, u32[]{:S(2)}) copy-start(f32[2048]{0:T(1024)} %param.26) | copy-start | bytes 24580
  199.1 0.7 copy-start.8
  199.7 0.7 copy-start.12
  200.4 2.4 %copy-start.1 = (f32[2048,128]{1,0:T(8,128)S(1)}, f32[2048,128]{1,0:T(8,128)}, u32[]{:S(2)}) copy-start(f32[2048,128]{1,0:T(8,128)} %get-tuple-element.66) | copy-start | bytes 3145732

commit v3 on v2

--- a/solution.py
+++ b/solution.py
@@ -18,6 +18,7 @@
 BF16 = jnp.bfloat16
 
 COL_MASS, COL_SIN, COL_GAIN, COL_SHARED, COL_NODE, COL_LINK, COL_COND = 0, 16, 48, 64, 72, 80, 88
+ABSENT = 2.0**20
 FLOW_G, FLOW_P, BACK_P, BACK_Q, SETUP, GRAM, LAST = range(7)
 
 
@@ -42,6 +43,8 @@
 def kernel(
     cap,
     width,
+    bucket_nodes,
+    bucket_cap,
     n_tm,
     n_dom,
     x0_ref,
@@ -56,7 +59,6 @@
     shared_diag_ref,
     node_ref,
     link_ref,
-    link_smem,
     cond_ref,
     amp_ref,
     phase_ref,
@@ -70,14 +72,15 @@
     p,
     q,
     fixed,
-    flow,
     g_parts,
     p_parts,
     flow_parts,
     slot_parts,
     blocks,
-    node_rows,
     node_cols,
+    bucket_rows,
+    scatter_parts,
+    shared_cols,
     pack,
     unpack,
     own,
@@ -99,6 +102,13 @@
     jump_send,
     jump_recv,
     value_send,
+    jump_sh_send,
+    jump_sh_recv,
+    value_sh_send,
+    pair_gain,
+    pair_jump,
+    pair_value,
+    value_recv,
     value_sh,
     send_sem,
     recv_sem,
@@ -108,7 +118,7 @@
     me_t, me_d = lax.axis_index("tm"), lax.axis_index("dom")
     nodes = x0_ref.shape[0]
     shard = w0_ref.shape[0] // n_dom
-    links = flow.shape[0]
+    links = flow_parts.shape[0]
     chunks, shard_chunks, link_chunks = nodes // LANES, shard // LANES, links // LANES
     at_sh, at_link = nodes, nodes + shard
     per_owner = width // LANES
@@ -148,6 +158,35 @@
             send_sem=tm_send.at[kind, step],
             recv_sem=tm_recv.at[kind, step],
             device_id={"tm": tm_peer(step)},
+            device_id_type=MESH,
+        )
+
+    pairs = n_tm // 2
+    core, chip = lax.rem(me_t, 2), me_t // 2
+
+    def pair_copy(kind, source, target):
+        return pltpu.make_async_remote_copy(
+            src_ref=source,
+            dst_ref=target,
+            send_sem=tm_send.at[4 + kind, 0],
+            recv_sem=tm_recv.at[4 + kind, 0],
+            device_id={"tm": me_t + 1 - 2 * core},
+            device_id_type=MESH,
+        )
+
+    def chip_peer(step):
+        return lax.rem(chip + step, pairs)
+
+    def chip_source(step):
+        return lax.rem(chip + pairs - step, pairs)
+
+    def chip_copy(kind, step, source, target):
+        return pltpu.make_async_remote_copy(
+            src_ref=source,
+            dst_ref=target,
+            send_sem=tm_send.at[kind, step],
+            recv_sem=tm_recv.at[kind, step],
+            device_id={"tm": 2 * chip_peer(step) + core},
             device_id_type=MESH,
         )
 
@@ -174,24 +213,68 @@
         table[COL_SHARED + a : COL_SHARED + a + 1, :] = shared_mass_ref[pl.ds(row, 1), :]
         table[COL_SHARED + 2 + a : COL_SHARED + 3 + a, :] = shared_diag_ref[pl.ds(row, 1), :]
         table[COL_SHARED + 4 + a : COL_SHARED + 5 + a, :] = gain_sh_ref[pl.ds(row, 1), :]
-    table[COL_NODE : COL_NODE + link_chunks, :] = node_ref[...].astype(F32)
-    table[COL_LINK : COL_LINK + link_chunks, :] = link_ref[...].astype(F32)
-    table[COL_COND : COL_COND + link_chunks, :] = cond_ref[...]
+    given = node_ref.shape[0]
+    table[COL_NODE : COL_NODE + given, :] = node_ref[...].astype(F32)
+    table[COL_LINK : COL_LINK + given, :] = link_ref[...].astype(F32)
+    table[COL_COND : COL_COND + given, :] = cond_ref[...]
     table_t[...] = table[...].T
 
     def column(at):
         return table_t[:, at : at + 1]
 
-    link_col = [column(COL_LINK + j).astype(jnp.int32) for j in range(link_chunks)]
-    link_row = [link_ref[j : j + 1, :] for j in range(link_chunks)]
+    nbuckets = nodes // bucket_nodes
+    bucket_rows[...] = jnp.zeros(bucket_rows.shape, F32)
+    crowd = jnp.zeros((1, 1), F32)
+    if nbuckets == 1:
+        for j in range(given):
+            across = slice(LANES * j, LANES * (j + 1))
+            bucket_rows[0, 0:1, across] = node_ref[j : j + 1, :].astype(F32)
+            bucket_rows[0, 1:2, across] = cond_ref[j : j + 1, :]
+        table[0:given, :] = node_ref[...].astype(F32)
+        table[8 : 8 + given, :] = link_ref[...].astype(F32)
+        table[16 : 16 + given, :] = cond_ref[...]
+    else:
+        given_node = [column(COL_NODE + j) for j in range(given)]
+        given_link = [column(COL_LINK + j) for j in range(given)]
+        given_cond = [column(COL_COND + j) for j in range(given)]
+        bucket_col = [v.astype(jnp.int32) // bucket_nodes for v in given_node]
+        bucket_row = [node_ref[j : j + 1, :] // bucket_nodes for j in range(given)]
+        place = []
+        for j in range(given):
+            rank = jnp.zeros((LANES, 1), F32)
+            for i in range(j + 1):
+                same = bucket_col[j] == bucket_row[i]
+                if i == j:
+                    same = same & (iota1 < iota0)
+                rank += jnp.sum(jnp.where(same, 1.0, 0.0), axis=1, keepdims=True)
+            crowd = jnp.maximum(crowd, jnp.max(rank, axis=0, keepdims=True))
+            place.append((bucket_col[j], rank.astype(jnp.int32)))
+
+        def picked(masks, values, none):
+            total = jnp.zeros((1, LANES), F32)
+            for mask, value in zip(masks, values):
+                total += jnp.sum(jnp.where(mask, value + none, 0.0), axis=0, keepdims=True)
+            return total - none
+
+        for i in range(nbuckets):
+            masks = [(b == i) & (iota1 == r) for b, r in place]
+            bucket_rows[i, 0:1, :] = picked(masks, given_node, ABSENT)
+            bucket_rows[i, 1:2, :] = picked(masks, given_cond, 0.0)
+        for i in range(link_chunks):
+            masks = [(iota1 + LANES * i) == b * bucket_cap + r for b, r in place]
+            table[i : i + 1, :] = picked(masks, given_node, ABSENT)
+            table[8 + i : 9 + i, :] = picked(masks, given_link, ABSENT)
+            table[16 + i : 17 + i, :] = picked(masks, given_cond, 0.0)
+    table2_t[...] = table[...].T
+
+    link_col = [table2_t[:, 8 + j : 9 + j].astype(jnp.int32) for j in range(link_chunks)]
+    link_row = [table[8 + j : 9 + j, :].astype(jnp.int32) for j in range(link_chunks)]
     if cap == width:
         slot_col, slot_row = link_col, link_row
-        crowd = jnp.zeros((1, LANES), F32)
     else:
         owner_col = [v // shard for v in link_col]
         owner_row = [v // shard for v in link_row]
         slot_col, slot_row = [], []
-        crowd = jnp.zeros((1, LANES), F32)
         for j in range(link_chunks):
             rank_row = jnp.zeros((1, LANES), F32)
             rank_col = jnp.zeros((LANES, 1), F32)
@@ -203,9 +286,11 @@
                     same_col = same_col & (iota1 < iota0)
                 rank_row += jnp.sum(jnp.where(same_row, 1.0, 0.0), axis=0, keepdims=True)
                 rank_col += jnp.sum(jnp.where(same_col, 1.0, 0.0), axis=1, keepdims=True)
-            crowd = jnp.maximum(crowd, rank_row)
+            real = jnp.where(owner_col[j] >= 0, rank_col, 0.0)
+            crowd = jnp.maximum(crowd, jnp.max(real, axis=0, keepdims=True))
             slot_row.append(owner_row[j] * width + rank_row.astype(jnp.int32))
             slot_col.append(owner_col[j] * width + rank_col.astype(jnp.int32))
+    link_cond_col = [table2_t[:, 16 + j : 17 + j] for j in range(link_chunks)]
     set_send[...] = jnp.zeros(set_send.shape, F32)
     for i in range(n_dom * per_owner):
         held = jnp.full((1, LANES), -1.0, F32)
@@ -214,7 +299,7 @@
             here = (iota1 + LANES * i) == slot_col[j]
             local = (link_col[j] % shard).astype(F32)
             held = jnp.maximum(held, jnp.max(jnp.where(here, local, -1.0), axis=0, keepdims=True))
-            total += jnp.sum(jnp.where(here, column(COL_COND + j), 0.0), axis=0, keepdims=True)
+            total += jnp.sum(jnp.where(here, link_cond_col[j], 0.0), axis=0, keepdims=True)
             unpack[LANES * j : LANES * (j + 1), LANES * i : LANES * (i + 1)] = ones_where(here)
             pack[LANES * i : LANES * (i + 1), LANES * j : LANES * (j + 1)] = ones_where(
                 (iota0 + LANES * i) == slot_row[j]
@@ -223,10 +308,11 @@
         set_send[o, h : h + 1, :] = held
         set_send[o, 2 + h : 3 + h, :] = total
     for o in range(n_dom):
-        set_send[o, 4:5, :] = crowd
+        set_send[o, 4:5, :] = jnp.broadcast_to(crowd, (1, LANES))
     gain_send[...] = jnp.zeros(gain_send.shape, F32)
     for m in range(n_tm):
-        gain_send[m, 0:1, :] = gain_in_ref[m : m + 1, :]
+        chunk = pairs * (m % 2) + m // 2
+        gain_send[m, 0:1, :] = gain_in_ref[chunk : chunk + 1, :]
         row = shard_chunks * me_d + m * shard_chunks // n_tm
         gain_send[m, 1:2, :] = gain_sh_ref[pl.ds(row, 1), :]
 
@@ -235,29 +321,39 @@
         dom_copy(SETUP, step, set_send.at[dom_peer(step)], set_recv.at[me_d]).start()
     for step in range(1, n_tm):
         tm_copy(0, step, gain_send.at[tm_peer(step)], gain_recv.at[me_t]).start()
+    pair_copy(0, gain_in_ref.at[pl.ds(pairs * (1 - core), pairs)], pair_gain).start()
     set_recv[me_d] = set_send[me_d]
     gain_recv[me_t] = gain_send[me_t]
 
+    lanes_of = lax.broadcasted_iota(jnp.int32, (LANES, bucket_nodes), 1)
     for j in range(link_chunks):
-        node_row = node_ref[j : j + 1, :]
-        node_col = column(COL_NODE + j).astype(jnp.int32)
-        link_cond[LANES * j : LANES * (j + 1), :] = jnp.broadcast_to(column(COL_COND + j), (LANES, LANES))
         across = slice(LANES * j, LANES * (j + 1))
-
-        def select(i, carry):
-            base = pl.multiple_of(i * LANES, LANES)
-            node_rows[pl.ds(base, LANES), across] = ones_where(iota0 + base == node_row)
-            node_cols[across, pl.ds(base, LANES)] = ones_where(iota1 + base == node_col)
-            return carry
-
-        lax.fori_loop(0, chunks, select, 0, unroll=2)
+        node_col = table2_t[:, j : j + 1].astype(jnp.int32)
+        local = jnp.where(node_col >= 0, node_col % bucket_nodes, -1)
+        node_cols[across, :] = ones_where(lanes_of == local)
+        link_cond[across, :] = jnp.broadcast_to(link_cond_col[j], (LANES, LANES))
         mass_sum = jnp.zeros((LANES, LANES), F32)
         for i in range(w0_ref.shape[0] // LANES):
-            mass_sum += jnp.where(iota1 + LANES * i == link_col[j], shared_mass_ref[i : i + 1, :], 0.0)
+            here = iota1 + LANES * i == link_col[j]
+            mass_sum += jnp.where(here, shared_mass_ref[i : i + 1, :], 0.0)
+            shared_cols[across, LANES * i : LANES * (i + 1)] = ones_where(here)
         link_mass[across, :] = jnp.broadcast_to(jnp.sum(mass_sum, axis=1, keepdims=True), (LANES, LANES))
+    span = bucket_rows.shape[2]
+    block_iota = lax.broadcasted_iota(jnp.int32, (bsize, span), 0).astype(F32)
+    eye = lax.broadcasted_iota(jnp.int32, (bsize, bsize), 0) == lax.broadcasted_iota(jnp.int32, (bsize, bsize), 1)
+    scatter_parts[...] = jnp.zeros(scatter_parts.shape, BF16)
+    per_bucket = bucket_nodes // bsize
 
     def cut(b, carry):
-        blocks[b] = split(jnp.concatenate([jac_ref[b], off_ref[b]], axis=1))
+        held = bucket_rows[b // per_bucket]
+        here = (block_iota + (b * bsize).astype(F32)) == held[0:1, :]
+        own_cond = jnp.sum(jnp.where(here, held[1:2, :], 0.0), axis=1, keepdims=True)
+        both = jnp.concatenate([jac_ref[b] + jnp.where(eye, own_cond, 0.0), off_ref[b]], axis=1)
+        parts = split(both)
+        blocks[b, :bsize, : 2 * bsize] = parts[:, :LANES]
+        blocks[b, bsize:, : 2 * bsize] = parts[:, LANES:]
+        blocks[b, :bsize, 2 * bsize :] = ones_where(here)
+        blocks[b, bsize:, 2 * bsize :] = jnp.zeros((bsize, span), BF16)
         return carry
 
     lax.fori_loop(0, nblocks, cut, 0, unroll=2)
@@ -274,11 +370,7 @@
     lax.fori_loop(0, chunks, begin, 0)
     x[at_sh : at_sh + shard, :] = w0_ref[rows(me_d * shard, shard), :]
 
-    def fetch(l, carry):
-        x[pl.ds(at_link + l, 1), :] = w0_ref[pl.ds(link_smem[l // LANES, lax.rem(l, LANES)], 1), :]
-        return carry
-
-    lax.fori_loop(0, links, fetch, 0, unroll=8)
+    x[at_link:, :] = halves(dot(shared_cols[...], split(w0_ref[...])))
 
     for step in range(1, n_dom):
         dom_copy(SETUP, step, set_send.at[dom_peer(step)], set_recv.at[dom_source(step)]).wait_recv()
@@ -307,34 +399,32 @@
         diag_sh[LANES * a : LANES * (a + 1), :] = jnp.broadcast_to(total, (LANES, LANES))
     flag_ref[...] = jnp.broadcast_to(crowd, flag_ref.shape)
 
-    def apply_blocks(parts, out):
+    def apply(vec, parts, out, shifted=None):
+        for t in range(nbuckets):
+            at = slice(t * bucket_cap, (t + 1) * bucket_cap)
+            flows = link_cond[at, :] * vec[at_link + at.start : at_link + at.stop, :]
+            scatter_parts[t, :bucket_cap, :] = split(-flows)
+
         def one(b, carry):
             other = block_link_ref[b]
-            mine, theirs = parts[b], parts[other]
-            acc = dot(blocks[b], jnp.concatenate([mine, theirs, mine, theirs], axis=0))
-            out[rows(b * bsize, bsize), :] = halves(acc)
+            at = rows(b * bsize, bsize)
+            acc = dot(blocks[b], jnp.concatenate([parts[b], parts[other], scatter_parts[b // per_bucket]], axis=0))
+            value = halves(acc[:bsize, :]) + acc[bsize:, :LANES]
+            if shifted is not None:
+                value = value - SHIFT * vec[at, :]
+                shifted[b] = split(value)
+            out[at, :] = value
             return carry
 
         lax.fori_loop(0, nblocks, one, 0, unroll=4)
 
     def gather_flow(parts):
-        flow[...] = halves(dot(node_cols[...], parts[...].reshape(nodes, 2 * LANES))) * link_cond[...]
-
-    def add_flow(vec, out, shift_by=None, parts=None):
-        flow_parts[...] = split(flow[...] - link_cond[...] * vec[at_link : at_link + links, :])
-        size = 2 * LANES
-
-        def one(i, carry):
-            at = rows(i * size, size)
-            value = out[at, :] + halves(dot(node_rows[at, :], flow_parts[...]))
-            if shift_by is not None:
-                value = value - SHIFT * shift_by[at, :]
-            out[at, :] = value
-            if parts is not None:
-                parts[pl.ds(i * 2 * each, 2 * each)] = split(value).reshape(2 * each, bsize, 2 * LANES)
-            return carry
-
-        lax.fori_loop(0, nodes // size, one, 0)
+        blocks_in = bucket_nodes // bsize
+        for t in range(nbuckets):
+            at = slice(t * bucket_cap, (t + 1) * bucket_cap)
+            chunk = parts[t * blocks_in : (t + 1) * blocks_in].reshape(bucket_nodes, 2 * LANES)
+            value = halves(dot(node_cols[at, :], chunk)) * link_cond[at, :]
+            flow_parts[at, :] = split(value)
 
     def start_exchange(kind):
         for step in range(1, n_dom):
@@ -359,15 +449,20 @@
             else:
                 copy.wait_send()
 
-    def send_flow(kind):
-        flow_parts[...] = split(flow[...])
-
-        def one(o, carry):
-            stage[kind, o] = halves(dot(pack[rows(o * width, width), :], flow_parts[...]))
+    def fill_stage(kind, matrix, value_parts):
+        some = n_dom // 2
+
+        def one(i, carry):
+            got = halves(dot(matrix[rows(i * some * width, some * width), :], value_parts))
+            stage[kind, pl.ds(i * some, some)] = got.reshape(some, width, LANES)
             return carry
 
-        lax.fori_loop(0, n_dom, one, 0)
+        lax.fori_loop(0, 2, one, 0)
         start_exchange(kind)
+
+    def send_flow(kind, parts):
+        gather_flow(parts)
+        fill_stage(kind, pack, flow_parts[...])
 
     def load_slots(kind):
         for o in range(n_dom):
@@ -379,14 +474,7 @@
         return halves(dot(own[...], slot_parts[...]))
 
     def send_back(kind, value):
-        value_parts = split(value)
-
-        def one(o, carry):
-            stage[kind, o] = halves(dot(own_t[rows(o * width, width), :], value_parts))
-            return carry
-
-        lax.fori_loop(0, n_dom, one, 0)
-        start_exchange(kind)
+        fill_stage(kind, own_t, split(value))
 
     def take_back(kind, out):
         wait_exchange(kind, True)
@@ -403,7 +491,7 @@
             fixed[at, :] = column(COL_SHARED + a) * x[at, :]
         fixed[at_link:, :] = link_mass[...] * x[at_link:, :]
 
-    def new_residual():
+    def residual_nodes():
         def one(i, carry):
             at = rows(i * LANES, LANES)
             value = fixed[at, :] - jx[at, :] - nonlin_ref[...] * jnp.tanh(x[at, :])
@@ -412,50 +500,57 @@
             return carry
 
         lax.fori_loop(0, chunks, one, 0)
-        g[nodes:, :] = fixed[nodes:, :] - jx[nodes:, :]
-
-    gather_flow(g_parts)
-    send_flow(FLOW_G)
-    apply_blocks(g_parts, jx)
-    add_flow(x, jx)
-    set_fixed(0)
+
     at = slice(at_sh, at_sh + shard)
-    wait_exchange(FLOW_G, False)
-    jx[at, :] = diag_sh[...] * x[at, :] - collect_flow(FLOW_G)
-    send_back(BACK_P, jx[at, :])
-    take_back(BACK_P, jx)
-    wait_exchange(BACK_P, False)
-    new_residual()
-
-    def gram_row(index, total):
-        return total[index : index + 1, :]
-
-    def newton(turn, carry):
-        gather_flow(g_parts)
-        send_flow(FLOW_G)
-        apply_blocks(g_parts, p)
-        add_flow(g, p, g, p_parts)
-        gather_flow(p_parts)
-        send_flow(FLOW_P)
-        apply_blocks(p_parts, q)
+
+    def residual_shared(where):
+        g[where, :] = fixed[where, :] - jx[where, :]
+
+    def shifted_shared():
         p[at, :] = (diag_sh[...] - SHIFT) * g[at, :] - collect_flow(FLOW_G)
         send_back(BACK_P, p[at, :])
-        q[at, :] = diag_sh[...] * p[at, :] - collect_flow(FLOW_P)
-        send_back(BACK_Q, q[at, :])
-        take_back(BACK_P, p)
-        add_flow(p, q)
-
-        def gram(i, sums):
-            here = rows(i * LANES, LANES)
-            vg, vp, vq = g[here, :], p[here, :], q[here, :]
-            pairs = ((vg, vg), (vg, vp), (vp, vp), (vg, vq), (vp, vq), (vq, vq))
+
+    def start_shared():
+        jx[at, :] = diag_sh[...] * x[at, :] - collect_flow(FLOW_P)
+        send_back(BACK_Q, jx[at, :])
+        residual_shared(at)
+        shifted_shared()
+        take_back(BACK_Q, jx)
+        residual_shared(slice(at_link, at_link + links))
+        for kind in (FLOW_P, BACK_Q):
+            wait_exchange(kind, False)
+
+    def newton(turn, carry):
+        send_flow(FLOW_G, g_parts)
+        pl.when(turn == 0)(start_shared)
+        apply(g, g_parts, p, p_parts)
+        send_flow(FLOW_P, p_parts)
+        pl.when(turn > 0)(shifted_shared)
+
+        def sum_over(i, sums, pairs):
             return tuple(
                 s + jnp.sum((a * b).reshape(LANES // 8, 8, LANES), axis=0)
                 for s, (a, b) in zip(sums, pairs)
             )
 
-        zero = jnp.zeros((8, LANES), F32)
-        sums = lax.fori_loop(0, chunks + shard_chunks, gram, (zero,) * 6)
+        def gram_early(i, sums):
+            here = rows(i * LANES, LANES)
+            vg, vp = g[here, :], p[here, :]
+            return sum_over(i, sums, ((vg, vg), (vg, vp), (vp, vp)))
+
+        def gram_late(i, sums):
+            here = rows(i * LANES, LANES)
+            vg, vp, vq = g[here, :], p[here, :], q[here, :]
+            return sum_over(i, sums, ((vg, vq), (vp, vq), (vq, vq)))
+
+        zero = (jnp.zeros((8, LANES), F32),) * 3
+        early = lax.fori_loop(0, chunks + shard_chunks, gram_early, zero)
+        q[at, :] = diag_sh[...] * p[at, :] - collect_flow(FLOW_P)
+        send_back(BACK_Q, q[at, :])
+        take_back(BACK_P, p)
+        apply(p, p_parts, q)
+        late = lax.fori_loop(0, chunks + shard_chunks, gram_late, zero)
+        sums = early + late
         for i, s in enumerate(sums):
             gram_send[i : i + 1, :] = jnp.sum(s, axis=0, keepdims=True)
         gram_send[6:8, :] = jnp.zeros((2, LANES), F32)
@@ -521,72 +616,107 @@
 
         @pl.when(turn < FINE * NEWTON - 1)
         def _():
-            new_residual()
+            residual_nodes()
+            residual_shared(slice(at_sh, at_link + links))
 
         return carry
 
+    send_flow(FLOW_P, g_parts)
+    apply(x, g_parts, jx)
+    set_fixed(0)
+    residual_nodes()
     lax.fori_loop(0, FINE * NEWTON, newton, 0)
 
     per_rows, per_shared = nodes // n_tm, shard // n_tm
-    for i in range(chunks):
-        here = slice(LANES * i, LANES * (i + 1))
-        jump_send[i, :per_rows, :] = x[here, :] - column(COL_GAIN + i) * x0_ref[here, :]
     for a in range(shard_chunks):
         here = slice(at_sh + LANES * a, at_sh + LANES * (a + 1))
         start = w0_ref[rows(me_d * shard + LANES * a, LANES), :]
         jump = x[here, :] - column(COL_SHARED + 4 + a) * start
         pieces = LANES // per_shared
         for m in range(pieces):
-            jump_send[a * pieces + m, per_rows:, :] = jump[per_shared * m : per_shared * (m + 1), :]
+            jump_sh_send[a * pieces + m] = jump[per_shared * m : per_shared * (m + 1), :]
     for step in range(1, n_tm):
-        tm_copy(1, step, jump_send.at[tm_peer(step)], jump_recv.at[me_t]).start()
-    jump_recv[me_t] = jump_send[me_t]
+        tm_copy(3, step, jump_sh_send.at[tm_peer(step)], jump_sh_recv.at[me_t]).start()
+    jump_sh_recv[me_t] = jump_sh_send[me_t]
+    for i in range(chunks):
+        here = slice(LANES * i, LANES * (i + 1))
+        jump_send[i] = x[here, :] - column(COL_GAIN + i) * x0_ref[here, :]
+    pair_copy(1, jump_send.at[pl.ds(pairs * (1 - core), pairs)], pair_jump).start()
+    pair_copy(0, gain_in_ref.at[pl.ds(pairs * (1 - core), pairs)], pair_gain).wait_recv()
     for step in range(1, n_tm):
         tm_copy(0, step, gain_send.at[tm_peer(step)], gain_recv.at[tm_source(step)]).wait_recv()
     for m in range(n_tm):
         table[m : m + 1, :] = gain_recv[m, 0:1, :]
         table[n_tm + m : n_tm + m + 1, :] = gain_recv[m, 1:2, :]
+    first_core = core == 0
+    own_gain, other_gain = gain_in_ref[pl.ds(pairs * core, pairs), :], pair_gain[...]
+    table[2 * n_tm : 2 * n_tm + pairs, :] = jnp.where(first_core, own_gain, other_gain)
+    table[3 * n_tm : 3 * n_tm + pairs, :] = jnp.where(first_core, other_gain, own_gain)
     table2_t[...] = table[...].T
     my_shared = rows(lax.rem(me_t, LANES // per_shared) * per_shared, per_shared)
+
+    def map_copy(step, holder):
+        return chip_copy(1, step, value_send.at[chip_peer(step)], jump_recv.at[holder])
+
+    def value_copy(step, holder):
+        return chip_copy(2, step, jump_recv.at[pairs + chip_peer(step)], value_recv.at[holder])
+
+    def shared_copy(step, holder):
+        return tm_copy(
+            7, step, value_sh_send.at[tm_peer(step)], value_sh.at[rows(holder * per_shared, per_shared)]
+        )
+
+    def solve(gains, jumps, values):
+        whole, total = gains[0], jumps[0]
+        for m in range(1, len(gains)):
+            whole = whole * gains[m]
+            total = gains[m] * total + jumps[m]
+        value = total / (1.0 - whole)
+        for m in range(len(gains)):
+            values[m] = value
+            if m + 1 < len(gains):
+                value = gains[m] * value + jumps[m]
+
+    def pair_slices(i):
+        mine, other = jump_send[pairs * core + i], pair_jump[i]
+        return jnp.where(first_core, mine, other), jnp.where(first_core, other, mine)
+
+    pair_copy(1, jump_send.at[pl.ds(pairs * (1 - core), pairs)], pair_jump).wait_recv()
+    for i in range(pairs):
+        first, second = pair_slices(i)
+        value_send[i] = table2_t[:, 3 * n_tm + i : 3 * n_tm + i + 1] * first + second
+    for step in range(1, pairs):
+        map_copy(step, chip).start()
+    jump_recv[chip] = value_send[chip]
     for step in range(1, n_tm):
-        tm_copy(1, step, jump_send.at[tm_peer(step)], jump_recv.at[tm_source(step)]).wait_recv()
-    for part, gains in (
-        (slice(0, per_rows), [table2_t[:, m : m + 1] for m in range(n_tm)]),
-        (
-            slice(per_rows, per_rows + per_shared),
-            [table2_t[my_shared, n_tm + m : n_tm + m + 1] for m in range(n_tm)],
-        ),
-    ):
-        whole, total = gains[0], jump_recv[0, part, :]
-        for m in range(1, n_tm):
-            whole = whole * gains[m]
-            total = gains[m] * total + jump_recv[m, part, :]
-        value = total / (1.0 - whole)
-        for m in range(n_tm):
-            value_send[m, part, :] = value
-            if m + 1 < n_tm:
-                value = gains[m] * value + jump_recv[m, part, :]
-
-    def value_copy(step, holder):
-        source = value_send.at[tm_peer(step), pl.ds(0, per_rows)]
-        return tm_copy(2, step, source, out_in_ref.at[rows(holder * per_rows, per_rows)])
-
-    def shared_copy(step, holder):
-        source = value_send.at[tm_peer(step), pl.ds(per_rows, per_shared)]
-        return tm_copy(3, step, source, value_sh.at[rows(holder * per_shared, per_shared)])
-
+        tm_copy(3, step, jump_sh_send.at[tm_peer(step)], jump_sh_recv.at[tm_source(step)]).wait_recv()
+    solve([table2_t[my_shared, n_tm + m : n_tm + m + 1] for m in range(n_tm)], jump_sh_recv, value_sh_send)
     for step in range(1, n_tm):
         shared_copy(step, me_t).start()
-        value_copy(step, me_t).start()
-    out_in_ref[rows(me_t * per_rows, per_rows), :] = value_send[me_t, :per_rows, :]
-    value_sh[rows(me_t * per_shared, per_shared), :] = value_send[me_t, per_rows:, :]
+    value_sh[rows(me_t * per_shared, per_shared), :] = value_sh_send[me_t]
+    for step in range(1, pairs):
+        map_copy(step, chip_source(step)).wait_recv()
+    pair_gains = [table2_t[:, 2 * k : 2 * k + 1] * table2_t[:, 2 * k + 1 : 2 * k + 2] for k in range(pairs)]
+    solve(pair_gains, jump_recv, jump_recv.at[pl.ds(pairs, pairs)])
+    for step in range(1, pairs):
+        value_copy(step, chip).start()
+    value_recv[chip] = jump_recv[pairs + chip]
     for step in range(1, n_tm):
         shared_copy(step, tm_source(step)).wait_recv()
     for step in range(1, n_dom):
         dom_copy(LAST, step, value_sh, out_sh_ref.at[rows(me_d * shard, shard)]).start()
     out_sh_ref[rows(me_d * shard, shard), :] = value_sh[...]
-    for step in range(1, n_tm):
-        value_copy(step, tm_source(step)).wait_recv()
+    for step in range(1, pairs):
+        value_copy(step, chip_source(step)).wait_recv()
+    half = nodes // 2
+    for i in range(pairs):
+        first, second = pair_slices(i)
+        even = value_recv[i]
+        odd = table2_t[:, 2 * n_tm + i : 2 * n_tm + i + 1] * even + first
+        out_in_ref[rows(half * core + LANES * i, LANES), :] = jnp.where(first_core, even, odd)
+        pair_value[LANES * i : LANES * (i + 1), :] = jnp.where(first_core, odd, even)
+    pair_copy(2, pair_value, out_in_ref.at[rows(half * core, half)]).start()
+    pair_copy(2, pair_value, out_in_ref.at[rows(half * (1 - core), half)]).wait_recv()
     for step in range(1, n_dom):
         copy = dom_copy(LAST, step, value_sh, out_sh_ref.at[rows(dom_source(step) * shard, shard)])
         copy.wait_recv()
@@ -594,29 +724,34 @@
         dom_copy(SETUP, step, set_send.at[dom_peer(step)], set_recv.at[me_d]).wait_send()
     for step in range(1, n_tm):
         tm_copy(0, step, gain_send.at[tm_peer(step)], gain_recv.at[me_t]).wait_send()
-        tm_copy(1, step, jump_send.at[tm_peer(step)], jump_recv.at[me_t]).wait_send()
+        tm_copy(3, step, jump_sh_send.at[tm_peer(step)], jump_sh_recv.at[me_t]).wait_send()
         shared_copy(step, me_t).wait_send()
-        value_copy(step, me_t).wait_send()
-
-
-def run(cap, width, collective_id, n_tm, n_dom, operands):
+    for step in range(1, pairs):
+        map_copy(step, chip).wait_send()
+        value_copy(step, chip).wait_send()
+    pair_copy(0, gain_in_ref.at[pl.ds(pairs * (1 - core), pairs)], pair_gain).wait_send()
+    pair_copy(1, jump_send.at[pl.ds(pairs * (1 - core), pairs)], pair_jump).wait_send()
+    pair_copy(2, pair_value, out_in_ref.at[rows(half * core, half)]).wait_send()
+
+
+def run(cap, width, bucket_nodes, bucket_cap, collective_id, n_tm, n_dom, operands):
     nodes, samples = operands[0].shape
     shared = operands[1].shape[0]
     shard = shared // n_dom
-    links = operands[10].shape[0] * operands[10].shape[1]
+    nbuckets = nodes // bucket_nodes
+    links = nbuckets * bucket_cap
+    span = -(-bucket_cap // LANES) * LANES
     nblocks, bsize = operands[4].shape[0], operands[4].shape[1]
     total = nodes + shard + links
     slots = n_dom * width
-    piece = (nodes + shard) // n_tm
     vmem = pl.BlockSpec(memory_space=pltpu.VMEM)
     smem = pl.BlockSpec(memory_space=pltpu.SMEM)
     specs = [vmem] * len(operands)
     specs[6] = smem
-    specs[12] = smem
     state = pltpu.VMEM((total, samples), F32)
     tile = pltpu.VMEM((LANES, LANES), F32)
     return pl.pallas_call(
-        functools.partial(kernel, cap, width, n_tm, n_dom),
+        functools.partial(kernel, cap, width, bucket_nodes, bucket_cap, n_tm, n_dom),
         out_shape=(
             jax.ShapeDtypeStruct((nodes, samples), F32),
             jax.ShapeDtypeStruct((shared, samples), F32),
@@ -631,14 +766,15 @@
             state,
             state,
             state,
-            pltpu.VMEM((links, samples), F32),
             pltpu.VMEM((nblocks, bsize, 2 * samples), BF16),
             pltpu.VMEM((nblocks, bsize, 2 * samples), BF16),
             pltpu.VMEM((links, 2 * samples), BF16),
             pltpu.VMEM((slots, 2 * samples), BF16),
-            pltpu.VMEM((nblocks, bsize, 4 * bsize), BF16),
-            pltpu.VMEM((nodes, links), BF16),
-            pltpu.VMEM((links, nodes), BF16),
+            pltpu.VMEM((nblocks, 2 * bsize, 2 * bsize + span), BF16),
+            pltpu.VMEM((links, bucket_nodes), BF16),
+            pltpu.VMEM((nbuckets, 8, span), F32),
+            pltpu.VMEM((nbuckets, span, 2 * samples), BF16),
+            pltpu.VMEM((links, shared), BF16),
             pltpu.VMEM((slots, links), BF16),
             pltpu.VMEM((links, slots), BF16),
             pltpu.VMEM((shard, slots), BF16),
@@ -657,14 +793,21 @@
             pltpu.VMEM((n_tm, 8, LANES), F32),
             pltpu.VMEM((8, LANES), F32),
             pltpu.VMEM((n_dom, 8, LANES), F32),
-            pltpu.VMEM((n_tm, piece, samples), F32),
-            pltpu.VMEM((n_tm, piece, samples), F32),
-            pltpu.VMEM((n_tm, piece, samples), F32),
+            pltpu.VMEM((n_tm, nodes // n_tm, samples), F32),
+            pltpu.VMEM((n_tm, nodes // n_tm, samples), F32),
+            pltpu.VMEM((n_tm, nodes // n_tm, samples), F32),
+            pltpu.VMEM((n_tm, shard // n_tm, samples), F32),
+            pltpu.VMEM((n_tm, shard // n_tm, samples), F32),
+            pltpu.VMEM((n_tm, shard // n_tm, samples), F32),
+            pltpu.VMEM((n_tm // 2, LANES), F32),
+            pltpu.VMEM((n_tm // 2, LANES, samples), F32),
+            pltpu.VMEM((nodes // 2, samples), F32),
+            pltpu.VMEM((n_tm // 2, LANES, samples), F32),
             pltpu.VMEM((shard, samples), F32),
             pltpu.SemaphoreType.DMA((7, n_dom)),
             pltpu.SemaphoreType.DMA((7, n_dom)),
-            pltpu.SemaphoreType.DMA((4, n_tm)),
-            pltpu.SemaphoreType.DMA((4, n_tm)),
+            pltpu.SemaphoreType.DMA((8, n_tm)),
+            pltpu.SemaphoreType.DMA((8, n_tm)),
         ],
         compiler_params=pltpu.CompilerParams(
             collective_id=collective_id, has_side_effects=True, vmem_limit_bytes=62 * 1024 * 1024
@@ -709,18 +852,17 @@
         lanes(shared_diag),
         lanes(link_node),
         lanes(link_shared),
-        lanes(link_shared),
         lanes(link_cond),
         source_amp,
         lanes(phase),
         lanes(nonlin),
     )
-    shard = state_shared.shape[1] // n_dom
-    new_in, new_sh, crowd = run(SLOTS, LANES, 0, n_tm, n_dom, operands)
+    nodes, shard = state_interior.shape[1], state_shared.shape[1] // n_dom
+    new_in, new_sh, crowd = run(SLOTS, LANES, 2 * LANES, SLOTS, 0, n_tm, n_dom, operands)
     new_in, new_sh = lax.cond(
         jnp.max(crowd) < SLOTS,
         lambda: (new_in, new_sh),
-        lambda: run(shard, shard, 1, n_tm, n_dom, operands)[:2],
+        lambda: run(shard, shard, nodes, link_node.shape[0], 1, n_tm, n_dom, operands)[:2],
     )
     return (new_in[None], new_sh[None])
 

time: 204 us -> 170 us (0.83)
  Pallas kernels: 196 us -> 163 us
    pallas_call x1, Pallas kernels: 196 us -> 163 us  [run(): pl.pallas_call(functools.partial(kernel, cap, width, bucket_nodes, bucket...]
where the time goes in v3:
time: 170 us
  Pallas kernels  163 us (96%)
  local copies, waits for them, and re-layouts  4.63 us (3%)
    pallas_call x1, Pallas kernels, run(): pl.pallas_call(functools.partial(kernel, cap, width, bucket_nodes, bucket...  163 us
    unnamed x28, local copies, waits for them, and re-layouts  4.63 us

profile of v3, /device:TPU:1, one launch (start us, length us, event | category | flops | bytes accessed | tf_op | source)
XLA Modules:
  0.0 169.9 jit_solution(17168823749802284373)
XLA Ops:
  0.6 0.0 copy-start.4
  0.6 0.0 copy-start.3
  0.7 0.0 copy-start.2
  0.7 0.0 copy-start.11
  0.7 0.7 copy-done.4
  1.3 0.0 copy-done.3
  1.3 0.0 copy-done.2
  1.4 0.0 copy-done.11
  1.4 0.0 copy-start
  1.4 0.0 copy-start.6
  1.4 0.0 copy-start.7
  1.4 0.0 copy-start.9
  1.4 0.0 copy-start.10
  1.4 162.5 %parareal.3 = (f32[2048,128]{1,0:T(8,128)}, f32[2048,128]{1,0:T(8,128)}, f32[8,128]{1,0:T(8,128)}) custom-call(f32[2048,128]{1,0:T(8,128)} %bitcast.14, f32[2048,128]{1,0:T(8,128)} %bitcast.16, f32[16,128]{1,0:T(8,128)S(1)} %bitcast.20, f32[16,128]{1,0:T(8,128)S(1)} %bitcast.22, f32[32,64,64]{2,1,0:T(8,128)} %jac_ref.1, f32[32,64,64]{2,1,0:T(8,128)} %off_ref.1, ...), custom_call_target="tpu_custom_call" | custom-call | tf_op jit(solution)/shard_map/parareal/pallas_call | solution.py:753
  163.9 0.0 copy-start.5
  163.9 1.3 reduce_max.9
  165.2 0.0 copy-start.8
  165.9 0.0 copy-start.12
  165.9 0.0 copy-done
  165.9 0.0 copy-done.6
  165.9 0.0 copy-done.7
  165.9 0.0 copy-done.9
  166.0 0.0 copy-done.10
  166.0 0.0 copy-done.5
  166.0 0.0 copy-done.8
  166.0 0.6 copy-done.12
  166.6 0.0 copy-start.1
  166.6 2.4 %copy.24 = f32[1,2048,128]{2,1,0:T(8,128)} copy(f32[1,2048,128]{2,1,0:T(8,128)} %bitcast.18) | data formatting | bytes 2097152
  168.9 0.0 copy-done.1
  168.9 1.0 copy.25
  (1 shorter events, 0.0 us)
Async XLA Ops:
  0.6 0.7 copy-start.4
  0.6 0.7 copy-start.3
  0.7 0.7 copy-start.2
  0.7 0.7 copy-start.11
  1.4 164.6 %copy-start = (f32[1,2048,128]{2,1,0:T(8,128)S(1)}, f32[1,2048,128]{2,1,0:T(8,128)}, u32[]{:S(2)}) copy-start(f32[1,2048,128]{2,1,0:T(8,128)} %param.18) | copy-start | bytes 3145732
  1.4 164.6 %copy-start.6 = (f32[2048]{0:T(1024)S(1)}, f32[2048]{0:T(1024)}, u32[]{:S(2)}) copy-start(f32[2048]{0:T(1024)} %param.27) | copy-start | bytes 24580
  1.4 164.6 %copy-start.7 = (f32[2048]{0:T(1024)S(1)}, f32[2048]{0:T(1024)}, u32[]{:S(2)}) copy-start(f32[2048]{0:T(1024)} %param.32) | copy-start | bytes 24580
  1.4 164.6 %copy-start.9 = (s32[512]{0:T(512)S(1)}, s32[512]{0:T(512)}, u32[]{:S(2)}) copy-start(s32[512]{0:T(512)} %param.29) | copy-start | bytes 6148
  1.4 164.6 %copy-start.10 = (f32[512]{0:T(512)S(1)}, f32[512]{0:T(512)}, u32[]{:S(2)}) copy-start(f32[512]{0:T(512)} %param.30) | copy-start | bytes 6148
  163.9 2.0 %copy-start.5 = (f32[2048]{0:T(1024)S(1)}, f32[2048]{0:T(1024)}, u32[]{:S(2)}) copy-start(f32[2048]{0:T(1024)} %param.26) | copy-start | bytes 24580
  165.2 0.7 copy-start.8
  165.9 0.7 copy-start.12
  166.6 2.4 %copy-start.1 = (f32[2048,128]{1,0:T(8,128)S(1)}, f32[2048,128]{1,0:T(8,128)}, u32[]{:S(2)}) copy-start(f32[2048,128]{1,0:T(8,128)} %get-tuple-element.65) | copy-start | bytes 3145732

commit v4 on v3

--- a/solution.py
+++ b/solution.py
@@ -47,12 +47,12 @@
     bucket_cap,
     n_tm,
     n_dom,
-    x0_ref,
-    w0_ref,
+    x0_hbm,
+    w0_hbm,
     gain_in_ref,
     gain_sh_ref,
-    jac_ref,
-    off_ref,
+    jac_hbm,
+    off_hbm,
     block_link_ref,
     mass_ref,
     shared_mass_ref,
@@ -60,12 +60,18 @@
     node_ref,
     link_ref,
     cond_ref,
-    amp_ref,
+    amp_hbm,
     phase_ref,
     nonlin_ref,
     out_in_ref,
     out_sh_ref,
     flag_ref,
+    x0_ref,
+    w0_ref,
+    jac_ref,
+    off_ref,
+    amp_ref,
+    load_sem,
     x,
     jx,
     g,
@@ -78,6 +84,7 @@
     slot_parts,
     blocks,
     node_cols,
+    node_rows,
     bucket_rows,
     scatter_parts,
     shared_cols,
@@ -189,6 +196,24 @@
             device_id={"tm": 2 * chip_peer(step) + core},
             device_id_type=MESH,
         )
+
+    far_first = sorted(range(1, n_dom), key=lambda step: (step % 2 == 0, abs(2 * step - n_dom)))
+    far_chips = sorted(range(1, pairs), key=lambda step: (step % 2 == 0, abs(2 * step - pairs)))
+
+    loads = [
+        pltpu.make_async_copy(source, target, load_sem.at[i])
+        for i, (source, target) in enumerate(
+            (
+                (jac_hbm, jac_ref),
+                (off_hbm, off_ref),
+                (x0_hbm, x0_ref),
+                (w0_hbm, w0_ref),
+                (amp_hbm, amp_ref),
+            )
+        )
+    ]
+    for load in loads:
+        load.start()
 
     if cap < width:
         for kind in range(4):
@@ -344,6 +369,9 @@
     scatter_parts[...] = jnp.zeros(scatter_parts.shape, BF16)
     per_bucket = bucket_nodes // bsize
 
+    for load in loads:
+        load.wait()
+
     def cut(b, carry):
         held = bucket_rows[b // per_bucket]
         here = (block_iota + (b * bsize).astype(F32)) == held[0:1, :]
@@ -352,7 +380,9 @@
         parts = split(both)
         blocks[b, :bsize, : 2 * bsize] = parts[:, :LANES]
         blocks[b, bsize:, : 2 * bsize] = parts[:, LANES:]
-        blocks[b, :bsize, 2 * bsize :] = ones_where(here)
+        places = ones_where(here)
+        blocks[b, :bsize, 2 * bsize :] = places
+        node_rows[rows(b * bsize, bsize), :] = places
         blocks[b, bsize:, 2 * bsize :] = jnp.zeros((bsize, span), BF16)
         return carry
 
@@ -397,13 +427,25 @@
     for a in range(shard_chunks):
         total = column(COL_SHARED + 2 + a) + jnp.sum(sums[a], axis=1, keepdims=True)
         diag_sh[LANES * a : LANES * (a + 1), :] = jnp.broadcast_to(total, (LANES, LANES))
-    flag_ref[...] = jnp.broadcast_to(crowd, flag_ref.shape)
-
-    def apply(vec, parts, out, shifted=None):
+    flag_ref[0, 0] = jnp.max(crowd)
+
+    def place_flows(vec):
         for t in range(nbuckets):
             at = slice(t * bucket_cap, (t + 1) * bucket_cap)
             flows = link_cond[at, :] * vec[at_link + at.start : at_link + at.stop, :]
             scatter_parts[t, :bucket_cap, :] = split(-flows)
+
+    def apply_blocks(parts, out):
+        def one(b, carry):
+            other = block_link_ref[b]
+            acc = dot(blocks[b, :, : 2 * bsize], jnp.concatenate([parts[b], parts[other]], axis=0))
+            out[rows(b * bsize, bsize), :] = halves(acc[:bsize, :]) + acc[bsize:, :LANES]
+            return carry
+
+        lax.fori_loop(0, nblocks, one, 0, unroll=4)
+
+    def apply(vec, parts, out, shifted=None):
+        place_flows(vec)
 
         def one(b, carry):
             other = block_link_ref[b]
@@ -427,7 +469,7 @@
             flow_parts[at, :] = split(value)
 
     def start_exchange(kind):
-        for step in range(1, n_dom):
+        for step in far_first:
             dom_copy(
                 kind,
                 step,
@@ -529,7 +571,7 @@
 
         def sum_over(i, sums, pairs):
             return tuple(
-                s + jnp.sum((a * b).reshape(LANES // 8, 8, LANES), axis=0)
+                s + jnp.sum((a * b).reshape(-1, 8, LANES), axis=0)
                 for s, (a, b) in zip(sums, pairs)
             )
 
@@ -538,25 +580,35 @@
             vg, vp = g[here, :], p[here, :]
             return sum_over(i, sums, ((vg, vg), (vg, vp), (vp, vp)))
 
-        def gram_late(i, sums):
-            here = rows(i * LANES, LANES)
+        size = 2 * LANES
+
+        def gram_late(here, sums):
             vg, vp, vq = g[here, :], p[here, :], q[here, :]
-            return sum_over(i, sums, ((vg, vq), (vp, vq), (vq, vq)))
+            return sum_over(0, sums, ((vg, vq), (vp, vq), (vq, vq)))
+
+        def place_and_gram(i, sums):
+            here = rows(i * size, size)
+            arriving = dot(node_rows[here, :], scatter_parts[i // (bucket_nodes // size)])
+            q[here, :] = q[here, :] + halves(arriving)
+            return gram_late(here, sums)
 
         zero = (jnp.zeros((8, LANES), F32),) * 3
         early = lax.fori_loop(0, chunks + shard_chunks, gram_early, zero)
+        apply_blocks(p_parts, q)
         q[at, :] = diag_sh[...] * p[at, :] - collect_flow(FLOW_P)
         send_back(BACK_Q, q[at, :])
+        late = gram_late(at, zero)
         take_back(BACK_P, p)
-        apply(p, p_parts, q)
-        late = lax.fori_loop(0, chunks + shard_chunks, gram_late, zero)
+        place_flows(p)
+        late = lax.fori_loop(0, nodes // size, place_and_gram, late)
         sums = early + late
         for i, s in enumerate(sums):
             gram_send[i : i + 1, :] = jnp.sum(s, axis=0, keepdims=True)
         gram_send[6:8, :] = jnp.zeros((2, LANES), F32)
-        for step in range(1, n_dom):
+        for step in far_first:
             dom_copy(GRAM, step, gram_send, gram_recv.at[me_d]).start()
         gram_recv[me_d] = gram_send[...]
+        take_back(BACK_Q, q)
         for kind in (FLOW_G, FLOW_P, BACK_P, BACK_Q):
             wait_exchange(kind, False)
         for step in range(1, n_dom):
@@ -607,7 +659,6 @@
             return carry
 
         lax.fori_loop(0, chunks + shard_chunks, one, 0)
-        take_back(BACK_Q, q)
         advance(slice(at_link, at_link + links))
 
         @pl.when(turn == NEWTON - 1)
@@ -685,7 +736,7 @@
     for i in range(pairs):
         first, second = pair_slices(i)
         value_send[i] = table2_t[:, 3 * n_tm + i : 3 * n_tm + i + 1] * first + second
-    for step in range(1, pairs):
+    for step in far_chips:
         map_copy(step, chip).start()
     jump_recv[chip] = value_send[chip]
     for step in range(1, n_tm):
@@ -698,12 +749,12 @@
         map_copy(step, chip_source(step)).wait_recv()
     pair_gains = [table2_t[:, 2 * k : 2 * k + 1] * table2_t[:, 2 * k + 1 : 2 * k + 2] for k in range(pairs)]
     solve(pair_gains, jump_recv, jump_recv.at[pl.ds(pairs, pairs)])
-    for step in range(1, pairs):
+    for step in far_chips:
         value_copy(step, chip).start()
     value_recv[chip] = jump_recv[pairs + chip]
     for step in range(1, n_tm):
         shared_copy(step, tm_source(step)).wait_recv()
-    for step in range(1, n_dom):
+    for step in far_first:
         dom_copy(LAST, step, value_sh, out_sh_ref.at[rows(me_d * shard, shard)]).start()
     out_sh_ref[rows(me_d * shard, shard), :] = value_sh[...]
     for step in range(1, pairs):
@@ -748,6 +799,8 @@
     smem = pl.BlockSpec(memory_space=pltpu.SMEM)
     specs = [vmem] * len(operands)
     specs[6] = smem
+    for i in (0, 1, 4, 5, 13):
+        specs[i] = pl.BlockSpec(memory_space=pl.ANY)
     state = pltpu.VMEM((total, samples), F32)
     tile = pltpu.VMEM((LANES, LANES), F32)
     return pl.pallas_call(
@@ -755,11 +808,17 @@
         out_shape=(
             jax.ShapeDtypeStruct((nodes, samples), F32),
             jax.ShapeDtypeStruct((shared, samples), F32),
-            jax.ShapeDtypeStruct((8, LANES), F32),
+            jax.ShapeDtypeStruct((1, 1), F32),
         ),
         in_specs=specs,
-        out_specs=(vmem, vmem, vmem),
+        out_specs=(vmem, vmem, smem),
         scratch_shapes=[
+            pltpu.VMEM((nodes, samples), F32),
+            pltpu.VMEM((shared, samples), F32),
+            pltpu.VMEM((nblocks, bsize, bsize), F32),
+            pltpu.VMEM((nblocks, bsize, bsize), F32),
+            pltpu.VMEM((nodes, samples), F32),
+            pltpu.SemaphoreType.DMA((5,)),
             state,
             state,
             state,
@@ -772,6 +831,7 @@
             pltpu.VMEM((slots, 2 * samples), BF16),
             pltpu.VMEM((nblocks, 2 * bsize, 2 * bsize + span), BF16),
             pltpu.VMEM((links, bucket_nodes), BF16),
+            pltpu.VMEM((nodes, span), BF16),
             pltpu.VMEM((nbuckets, 8, span), F32),
             pltpu.VMEM((nbuckets, span, 2 * samples), BF16),
             pltpu.VMEM((links, shared), BF16),
@@ -860,7 +920,7 @@
     nodes, shard = state_interior.shape[1], state_shared.shape[1] // n_dom
     new_in, new_sh, crowd = run(SLOTS, LANES, 2 * LANES, SLOTS, 0, n_tm, n_dom, operands)
     new_in, new_sh = lax.cond(
-        jnp.max(crowd) < SLOTS,
+        crowd[0, 0] < SLOTS,
         lambda: (new_in, new_sh),
         lambda: run(shard, shard, nodes, link_node.shape[0], 1, n_tm, n_dom, operands)[:2],
     )

time: 170 us -> 166 us (0.976)
  Pallas kernels: 163 us -> 159 us
    pallas_call x1, Pallas kernels: 163 us -> 159 us  [run(): pl.pallas_call(functools.partial(kernel, cap, width, bucket_nodes, bucket...]
where the time goes in v4:
time: 166 us; the launch traced here: 165 us
  Pallas kernels  159 us (96%)
  local copies, waits for them, and re-layouts  4.66 us (3%)
    pallas_call x1, Pallas kernels, run(): pl.pallas_call(functools.partial(kernel, cap, width, bucket_nodes, bucket...  159 us
    unnamed x28, local copies, waits for them, and re-layouts  4.66 us

profile of v4, /device:TPU:1, one launch (start us, length us, event | category | flops | bytes accessed | tf_op | source)
XLA Modules:
  0.0 165.4 jit_solution(10712528037600886250)
XLA Ops:
  0.6 0.0 copy-start.4
  0.6 0.0 copy-start.3
  0.7 0.0 copy-start.2
  0.7 0.0 copy-start.11
  0.7 0.7 copy-done.4
  1.3 0.0 copy-done.3
  1.3 0.0 copy-done.2
  1.4 0.0 copy-done.11
  1.4 0.0 copy-start
  1.4 0.0 copy-start.6
  1.4 0.0 copy-start.7
  1.4 0.0 copy-start.9
  1.4 0.0 copy-start.10
  1.4 159.3 %parareal.3 = (f32[2048,128]{1,0:T(8,128)}, f32[2048,128]{1,0:T(8,128)}, f32[1,1]{1,0:T(1,128)}) custom-call(f32[2048,128]{1,0:T(8,128)} %bitcast.15, f32[2048,128]{1,0:T(8,128)} %bitcast.17, f32[16,128]{1,0:T(8,128)S(1)} %bitcast.21, f32[16,128]{1,0:T(8,128)S(1)} %bitcast.23, f32[32,64,64]{2,1,0:T(8,128)} %jac_hbm.1, f32[32,64,64]{2,1,0:T(8,128)} %off_hbm.1, ...), custom_call_target="tpu_custom_call" | custom-call | tf_op jit(solution)/shard_map/parareal/pallas_call | solution.py:806
  160.7 0.0 copy-start.5
  161.4 0.0 copy-start.8
  161.4 0.0 copy-start.12
  161.4 0.0 copy-done
  161.4 0.0 copy-done.6
  161.4 0.0 copy-done.7
  161.5 0.0 copy-done.9
  161.5 0.0 copy-done.10
  161.5 0.0 copy-done.5
  161.5 0.6 copy-done.8
  162.1 0.0 copy-done.12
  162.1 0.0 copy-start.1
  162.1 2.4 %copy.24 = f32[1,2048,128]{2,1,0:T(8,128)} copy(f32[1,2048,128]{2,1,0:T(8,128)} %bitcast.19) | data formatting | bytes 2097152
  164.4 0.0 copy-done.1
  164.4 1.0 copy.25
  (1 shorter events, 0.0 us)
Async XLA Ops:
  0.6 0.7 copy-start.4
  0.6 0.7 copy-start.3
  0.7 0.7 copy-start.2
  0.7 0.7 copy-start.11
  1.4 160.1 %copy-start = (f32[1,2048,128]{2,1,0:T(8,128)S(1)}, f32[1,2048,128]{2,1,0:T(8,128)}, u32[]{:S(2)}) copy-start(f32[1,2048,128]{2,1,0:T(8,128)} %param.18) | copy-start | bytes 3145732
  1.4 160.1 %copy-start.6 = (f32[2048]{0:T(1024)S(1)}, f32[2048]{0:T(1024)}, u32[]{:S(2)}) copy-start(f32[2048]{0:T(1024)} %param.27) | copy-start | bytes 24580
  1.4 160.1 %copy-start.7 = (f32[2048]{0:T(1024)S(1)}, f32[2048]{0:T(1024)}, u32[]{:S(2)}) copy-start(f32[2048]{0:T(1024)} %param.32) | copy-start | bytes 24580
  1.4 160.1 %copy-start.9 = (s32[512]{0:T(512)S(1)}, s32[512]{0:T(512)}, u32[]{:S(2)}) copy-start(s32[512]{0:T(512)} %param.29) | copy-start | bytes 6148
  1.4 160.1 %copy-start.10 = (f32[512]{0:T(512)S(1)}, f32[512]{0:T(512)}, u32[]{:S(2)}) copy-start(f32[512]{0:T(512)} %param.30) | copy-start | bytes 6148
  160.7 0.8 copy-start.5
  161.4 0.7 copy-start.8
  161.4 0.7 copy-start.12
  162.1 2.4 %copy-start.1 = (f32[2048,128]{1,0:T(8,128)S(1)}, f32[2048,128]{1,0:T(8,128)}, u32[]{:S(2)}) copy-start(f32[2048,128]{1,0:T(8,128)} %get-tuple-element.65) | copy-start | bytes 3145732

commit v5 on v4

--- a/solution.py
+++ b/solution.py
@@ -541,7 +541,7 @@
             g_parts[pl.ds(i * each, each)] = split(value).reshape(each, bsize, 2 * LANES)
             return carry
 
-        lax.fori_loop(0, chunks, one, 0)
+        lax.fori_loop(0, chunks, one, 0, unroll=4)
 
     at = slice(at_sh, at_sh + shard)
 
@@ -600,7 +600,7 @@
         late = gram_late(at, zero)
         take_back(BACK_P, p)
         place_flows(p)
-        late = lax.fori_loop(0, nodes // size, place_and_gram, late)
+        late = lax.fori_loop(0, nodes // size, place_and_gram, late, unroll=2)
         sums = early + late
         for i, s in enumerate(sums):
             gram_send[i : i + 1, :] = jnp.sum(s, axis=0, keepdims=True)
@@ -658,7 +658,7 @@
             advance(rows(i * LANES, LANES))
             return carry
 
-        lax.fori_loop(0, chunks + shard_chunks, one, 0)
+        lax.fori_loop(0, chunks + shard_chunks, one, 0, unroll=3)
         advance(slice(at_link, at_link + links))
 
         @pl.when(turn == NEWTON - 1)

time: 166 us -> 162 us (0.976)
  Pallas kernels: 159 us -> 156 us
    pallas_call x1, Pallas kernels: 159 us -> 156 us  [run(): pl.pallas_call(functools.partial(kernel, cap, width, bucket_nodes, bucket...]
where the time goes in v5:
time: 162 us
  Pallas kernels  156 us (96%)
  local copies, waits for them, and re-layouts  4.66 us (3%)
    pallas_call x1, Pallas kernels, run(): pl.pallas_call(functools.partial(kernel, cap, width, bucket_nodes, bucket...  156 us
    unnamed x28, local copies, waits for them, and re-layouts  4.66 us

profile of v5, /device:TPU:1, one launch (start us, length us, event | category | flops | bytes accessed | tf_op | source)
XLA Modules:
  0.0 162.1 jit_solution(5110920718390715769)
XLA Ops:
  0.6 0.0 copy-start.4
  0.6 0.0 copy-start.3
  0.7 0.0 copy-start.2
  0.7 0.0 copy-start.11
  0.7 0.7 copy-done.4
  1.3 0.0 copy-done.3
  1.3 0.0 copy-done.2
  1.4 0.0 copy-done.11
  1.4 0.0 copy-start
  1.4 0.0 copy-start.6
  1.4 0.0 copy-start.7
  1.4 0.0 copy-start.9
  1.4 0.0 copy-start.10
  1.4 156.0 %parareal.3 = (f32[2048,128]{1,0:T(8,128)}, f32[2048,128]{1,0:T(8,128)}, f32[1,1]{1,0:T(1,128)}) custom-call(f32[2048,128]{1,0:T(8,128)} %bitcast.15, f32[2048,128]{1,0:T(8,128)} %bitcast.17, f32[16,128]{1,0:T(8,128)S(1)} %bitcast.21, f32[16,128]{1,0:T(8,128)S(1)} %bitcast.23, f32[32,64,64]{2,1,0:T(8,128)} %jac_hbm.1, f32[32,64,64]{2,1,0:T(8,128)} %off_hbm.1, ...), custom_call_target="tpu_custom_call" | custom-call | tf_op jit(solution)/shard_map/parareal/pallas_call | solution.py:806
  157.4 0.0 copy-start.5
  158.1 0.0 copy-start.8
  158.1 0.0 copy-start.12
  158.1 0.0 copy-done
  158.1 0.0 copy-done.6
  158.1 0.0 copy-done.7
  158.2 0.0 copy-done.9
  158.2 0.0 copy-done.10
  158.2 0.0 copy-done.5
  158.2 0.6 copy-done.8
  158.8 0.0 copy-done.12
  158.8 0.0 copy-start.1
  158.8 2.4 %copy.24 = f32[1,2048,128]{2,1,0:T(8,128)} copy(f32[1,2048,128]{2,1,0:T(8,128)} %bitcast.19) | data formatting | bytes 2097152
  161.1 0.0 copy-done.1
  161.1 1.0 copy.25
  (1 shorter events, 0.0 us)
Async XLA Ops:
  0.6 0.7 copy-start.4
  0.6 0.7 copy-start.3
  0.7 0.7 copy-start.2
  0.7 0.7 copy-start.11
  1.4 156.8 %copy-start = (f32[1,2048,128]{2,1,0:T(8,128)S(1)}, f32[1,2048,128]{2,1,0:T(8,128)}, u32[]{:S(2)}) copy-start(f32[1,2048,128]{2,1,0:T(8,128)} %param.18) | copy-start | bytes 3145732
  1.4 156.8 %copy-start.6 = (f32[2048]{0:T(1024)S(1)}, f32[2048]{0:T(1024)}, u32[]{:S(2)}) copy-start(f32[2048]{0:T(1024)} %param.27) | copy-start | bytes 24580
  1.4 156.8 %copy-start.7 = (f32[2048]{0:T(1024)S(1)}, f32[2048]{0:T(1024)}, u32[]{:S(2)}) copy-start(f32[2048]{0:T(1024)} %param.32) | copy-start | bytes 24580
  1.4 156.8 %copy-start.9 = (s32[512]{0:T(512)S(1)}, s32[512]{0:T(512)}, u32[]{:S(2)}) copy-start(s32[512]{0:T(512)} %param.29) | copy-start | bytes 6148
  1.4 156.8 %copy-start.10 = (f32[512]{0:T(512)S(1)}, f32[512]{0:T(512)}, u32[]{:S(2)}) copy-start(f32[512]{0:T(512)} %param.30) | copy-start | bytes 6148
  157.4 0.8 copy-start.5
  158.1 0.7 copy-start.8
  158.1 0.7 copy-start.12
  158.8 2.4 %copy-start.1 = (f32[2048,128]{1,0:T(8,128)S(1)}, f32[2048,128]{1,0:T(8,128)}, u32[]{:S(2)}) copy-start(f32[2048,128]{1,0:T(8,128)} %get-tuple-element.65) | copy-start | bytes 3145732
